TPU v7x, 32 devices: a whole 2x2x4 slice. The times are simulated.
32 devices in a mesh: shot: 2 (over core), gx: 4 (over y, x), gy: 4 (over z).
Axes of the slice: x: 2, y: 2, z: 4, core: 2. Of those that a mesh axis runs over, the one named last changes fastest.
Arguments:
- stress_fields: float32 [4, 3, 6, 64, 64, 128], P('shot', None, None, 'gx', 'gy'), may hold values from -6 to 6
- velocity_fields: float32 [4, 3, 3, 64, 64, 128], P('shot', None, None, 'gx', 'gy'), may hold values from -6 to 6
- lame: float32 [64, 64, 128], P('gx', 'gy'), may hold values from 0.4 to 1.6
- shear: float32 [64, 64, 128], P('gx', 'gy'), may hold values from 0.25 to 1
- density: float32 [64, 64, 128], P('gx', 'gy'), may hold values from 0.8 to 2
- lame_change: float32 [64, 64, 128], P('gx', 'gy'), may hold values from -3 to 3
- shear_change: float32 [64, 64, 128], P('gx', 'gy'), may hold values from -3 to 3
- density_change: float32 [64, 64, 128], P('gx', 'gy'), may hold values from -3 to 3
- source_cell: int32 [4], P('shot'), may hold values from 0 to 524287
- source_amp: float32 [4], P('shot'), may hold values from 4 to 16
- receiver_cell: int32 [4, 512], P('shot'), may hold values from 0 to 4095
Outputs:
- new_velocity: float32 [4, 2, 3, 64, 64, 128], P('shot', None, None, 'gx', 'gy')
- new_stress: float32 [4, 2, 6, 64, 64, 128], P('shot', None, None, 'gx', 'gy')
- kernels: float32 [3, 64, 64, 128], P(None, ('gx', 'shot'), 'gy')
Inputs may be any that keep to these rules, and one draw needn't show every extreme that they name: source_cell[s] = x * 64 * 128 + y * 128 + z for the source's grid cell (x, y, z). receiver_cell[s, r] = x * 64 + y for a receiver at (x, y, 2); several receivers of a shot may share a cell.
All inputs are finite; a program needn't handle non-finite values.
Results may differ from a plain program's by a relative error of at most 0.0003.
Values sent between devices are 32-bit elements; how exact they have to be, the bound alone decides.
A program may use at most 128 MiB of HBM per device.

v0:
```python
import jax
import jax.numpy as jnp
from jax import lax
from jax.sharding import PartitionSpec as P

RDEPTH = 2


courant = 0.25
stress_upper_rows = (0,)
stress_lower_rows = (3, 4)
stress_upper_columns = (1,)
stress_lower_columns = (3, 5)
motion_upper_rows = (1, 2)
motion_lower_rows = (0,)
motion_upper_columns = (0, 2)
motion_lower_columns = (1,)


def extended(cells, sides, width):
    for axis, dim in sides:
        count = lax.axis_size(axis)
        ends = count - 1
        head = lax.slice_in_dim(cells, 0, width, axis=dim)
        tail = lax.slice_in_dim(cells, cells.shape[dim] - width, cells.shape[dim], axis=dim)
        cells = jnp.concatenate(
            [
                lax.ppermute(tail, axis, [(i, (i + 1) % count) for i in range(ends)]),
                cells,
                lax.ppermute(head, axis, [((i + 1) % count, i) for i in range(ends)]),
            ],
            axis=dim,
        )
    return cells


def forward_rows(quantity, upper_face):
    return jnp.concatenate([quantity[..., 1:, :, :], upper_face], axis=-3) - quantity


def backward_rows(quantity, lower_face):
    return quantity - jnp.concatenate([lower_face, quantity[..., :-1, :, :]], axis=-3)


def forward_columns(quantity, upper_face):
    return jnp.concatenate([quantity[..., 1:, :], upper_face], axis=-2) - quantity


def backward_columns(quantity, lower_face):
    return quantity - jnp.concatenate([lower_face, quantity[..., :-1, :]], axis=-2)


def forward_depth(quantity):
    return (
        jnp.concatenate([quantity[..., 1:], jnp.zeros_like(quantity[..., :1])], axis=-1) - quantity
    )


def backward_depth(quantity):
    return quantity - jnp.concatenate(
        [jnp.zeros_like(quantity[..., :1]), quantity[..., :-1]], axis=-1
    )


def component(array, index):
    return array[..., index, :, :, :]


def wavefield(array, index):
    return array[..., index, :, :, :, :]


def accelerations(stress, upper_rows, lower_rows, upper_columns, lower_columns):
    accel_x = (
        forward_rows(component(stress, 0), component(upper_rows, 0))
        + backward_columns(component(stress, 3), component(lower_columns, 0))
        + backward_depth(component(stress, 4))
    )
    accel_y = (
        backward_rows(component(stress, 3), component(lower_rows, 0))
        + forward_columns(component(stress, 1), component(upper_columns, 0))
        + backward_depth(component(stress, 5))
    )
    accel_z = (
        backward_rows(component(stress, 4), component(lower_rows, 1))
        + backward_columns(component(stress, 5), component(lower_columns, 1))
        + forward_depth(component(stress, 2))
    )
    return jnp.stack([accel_x, accel_y, accel_z], axis=-4)


def strains(velocity, upper_rows, lower_rows, upper_columns, lower_columns):
    strain_xx = backward_rows(component(velocity, 0), component(lower_rows, 0))
    strain_yy = backward_columns(component(velocity, 1), component(lower_columns, 0))
    strain_zz = backward_depth(component(velocity, 2))
    shear_xy = forward_columns(component(velocity, 0), component(upper_columns, 0)) + forward_rows(
        component(velocity, 1), component(upper_rows, 0)
    )
    shear_xz = forward_depth(component(velocity, 0)) + forward_rows(
        component(velocity, 2), component(upper_rows, 1)
    )
    shear_yz = forward_depth(component(velocity, 1)) + forward_columns(
        component(velocity, 2), component(upper_columns, 1)
    )
    return jnp.stack([strain_xx, strain_yy, strain_zz, shear_xy, shear_xz, shear_yz], axis=-4)


def moduli(strain, first, second):
    trace = component(strain, 0) + component(strain, 1) + component(strain, 2)
    parts = [first * trace + 2.0 * second * component(strain, index) for index in range(3)]
    parts = parts + [second * component(strain, index) for index in range(3, 6)]
    return jnp.stack(parts, axis=-4)


def update_velocity(velocity, accel, buoyancy, density_change, source_field, record_field):
    scaled = courant * buoyancy
    base = wavefield(velocity, 0) + scaled * wavefield(accel, 0)
    base = base.at[..., 2, :, :, :].add(scaled * source_field)
    born = wavefield(velocity, 1) + scaled * (
        wavefield(accel, 1) - density_change * buoyancy * wavefield(accel, 0)
    )
    adjoint = wavefield(velocity, 2) + scaled * wavefield(accel, 2)
    adjoint = adjoint.at[..., 2, :, :, :].add(scaled * record_field * component(born, 2))
    return jnp.stack([base, born, adjoint], axis=-5)


def update_stress(stress, strain, lame, shear, lame_change, shear_change):
    born = wavefield(stress, 1) + courant * (
        moduli(wavefield(strain, 1), lame, shear)
        + moduli(wavefield(strain, 0), lame_change, shear_change)
    )
    adjoint = wavefield(stress, 2) + courant * moduli(wavefield(strain, 2), lame, shear)
    return jnp.stack([born, adjoint], axis=-5)


def kernel_terms(strain, new_stress, accel, velocity_next, buoyancy):
    base_strain = wavefield(strain, 0)
    adjoint_stress = wavefield(new_stress, 1)
    trace_product = (
        component(base_strain, 0) + component(base_strain, 1) + component(base_strain, 2)
    ) * (component(adjoint_stress, 0) + component(adjoint_stress, 1) + component(adjoint_stress, 2))
    shear_sum = 2.0 * (
        component(base_strain, 0) * component(adjoint_stress, 0)
        + component(base_strain, 1) * component(adjoint_stress, 1)
        + component(base_strain, 2) * component(adjoint_stress, 2)
    )
    shear_sum = (
        shear_sum
        + component(base_strain, 3) * component(adjoint_stress, 3)
        + component(base_strain, 4) * component(adjoint_stress, 4)
        + component(base_strain, 5) * component(adjoint_stress, 5)
    )
    density_sum = buoyancy * jnp.sum(wavefield(accel, 0) * wavefield(velocity_next, 2), axis=-4)
    return jnp.stack([trace_product, shear_sum, density_sum], axis=-4)


def select(fields, indices):
    return jnp.stack([fields[:, :, index] for index in indices], axis=2)


def rim_faces(padded, upper_rows, lower_rows, upper_columns, lower_columns):
    return (
        select(padded[:, :, :, -1:, 1:-1, :], upper_rows),
        select(padded[:, :, :, :1, 1:-1, :], lower_rows),
        select(padded[:, :, :, 1:-1, -1:, :], upper_columns),
        select(padded[:, :, :, 1:-1, :1, :], lower_columns),
    )


def point_fields(
    row_ids, column_ids, depth_ids, every_column, source_cell, source_amp, receiver_cell
):
    depth = depth_ids.shape[0]
    source_row = source_cell // (every_column * depth)
    source_column = source_cell // depth % every_column
    source_level = source_cell % depth
    row_hit = (source_row[:, None] == row_ids[None, :]).astype(jnp.float32)
    column_hit = (source_column[:, None] == column_ids[None, :]).astype(jnp.float32)
    level_hit = (source_level[:, None] == depth_ids[None, :]).astype(jnp.float32)
    source_field = (
        source_amp[:, None, None, None]
        * row_hit[:, :, None, None]
        * column_hit[:, None, :, None]
        * level_hit[:, None, None, :]
    )
    receiver_rows = receiver_cell // every_column
    receiver_columns = receiver_cell % every_column
    row_marks = (receiver_rows[:, :, None] == row_ids[None, None, :]).astype(jnp.float32)
    column_marks = (receiver_columns[:, :, None] == column_ids[None, None, :]).astype(jnp.float32)
    counts = jnp.einsum("sri,srj->sij", row_marks, column_marks, precision=lax.Precision.HIGHEST)
    plane = (depth_ids == RDEPTH).astype(jnp.float32)
    record_field = counts[:, :, :, None] * plane
    return (source_field, record_field)


def shards(
    stress_fields,
    velocity_fields,
    lame,
    shear,
    density,
    lame_change,
    shear_change,
    density_change,
    source_cell,
    source_amp,
    receiver_cell,
):
    rows, cols, depth = lame.shape
    every_column = cols * lax.axis_size("gy")
    row_start = lax.axis_index("gx") * rows
    column_start = lax.axis_index("gy") * cols
    depth_ids = jnp.arange(depth, dtype=jnp.int32)
    buoyancy = 1.0 / density
    row_ids = row_start + jnp.arange(rows, dtype=jnp.int32)
    column_ids = column_start + jnp.arange(cols, dtype=jnp.int32)
    source_field, record_field = point_fields(
        row_ids, column_ids, depth_ids, every_column, source_cell, source_amp, receiver_cell
    )
    padded_stress = extended(stress_fields, (("gx", 3), ("gy", 4)), 1)
    stress_faces = rim_faces(
        padded_stress,
        stress_upper_rows,
        stress_lower_rows,
        stress_upper_columns,
        stress_lower_columns,
    )
    accel = accelerations(stress_fields, *stress_faces)
    velocity_next = update_velocity(
        velocity_fields, accel, buoyancy, density_change, source_field, record_field
    )
    padded_motion = extended(velocity_next, (("gx", 3), ("gy", 4)), 1)
    motion_faces = rim_faces(
        padded_motion,
        motion_upper_rows,
        motion_lower_rows,
        motion_upper_columns,
        motion_lower_columns,
    )
    strain = strains(velocity_next, *motion_faces)
    new_stress = update_stress(stress_fields, strain, lame, shear, lame_change, shear_change)
    local_terms = jnp.sum(kernel_terms(strain, new_stress, accel, velocity_next, buoyancy), axis=0)
    owned = lax.psum_scatter(local_terms, "shot", scatter_dimension=1, tiled=True)
    total_shots = stress_fields.shape[0] * lax.axis_size("shot")
    return (velocity_next[:, 1:], new_stress, owned / total_shots)


def solution(mesh):
    return jax.shard_map(
        shards,
        mesh=mesh,
        in_specs=(
            P("shot", None, None, "gx", "gy", None),
            P("shot", None, None, "gx", "gy", None),
            P("gx", "gy", None),
            P("gx", "gy", None),
            P("gx", "gy", None),
            P("gx", "gy", None),
            P("gx", "gy", None),
            P("gx", "gy", None),
            P("shot"),
            P("shot"),
            P("shot", None),
        ),
        out_specs=(
            P("shot", None, None, "gx", "gy", None),
            P("shot", None, None, "gx", "gy", None),
            P(None, ("gx", "shot"), "gy", None),
        ),
        check_vma=False,
    )
```

profile of v0, /device:TPU:0, one launch (start us, length us, event | category | flops | bytes accessed | tf_op | source)
XLA Modules:
  0.0 123.5 jit_solution(5808959714331605270)
XLA Ops:
  7.2 1.1 fusion.51
  8.3 1.0 copy.116
  9.3 1.3 %collective-permute-start = (f32[2,3,6,1,16,128]{5,3,0,1,4,2:T(1,128)}, f32[2,3,6,1,16,128]{5,3,0,1,4,2:T(1,128)}, u32[]{:S(2)}, u32[]{:S(2)}) collective-permute-start(f32[2,3,6,1,16,128]{5,3,0,1,4,2:T(1,128)} %copy.116), channel_id=1, source_target_pairs={{4,0},{8,4},{12,8},{5,1},{9,5},{13,9},{6,2},{10,6},{14,10},{7,3},{... | collective-permute-start | bytes 884744 | tf_op jit(solution)/shard_map/ppermute | solution.py:30
  10.6 1.0 copy.119
  11.7 6.3 %collective-permute-start.1 = (f32[2,3,6,1,16,128]{5,3,0,1,4,2:T(1,128)}, f32[2,3,6,1,16,128]{5,3,0,1,4,2:T(1,128)}, u32[]{:S(2)}, u32[]{:S(2)}) collective-permute-start(f32[2,3,6,1,16,128]{5,3,0,1,4,2:T(1,128)} %copy.119), channel_id=1, source_target_pairs={{0,4},{4,8},{8,12},{1,5},{5,9},{9,13},{2,6},{6,10},{10,14},{3,7},{... | collective-permute-start | bytes 884744 | tf_op jit(solution)/shard_map/ppermute | solution.py:28
  18.0 2.8 %fusion.50 = (f32[2,3,1,16,16,128]{5,4,3,2,1,0:T(8,128)S(1)}, f32[2,3,1,16,16,128]{5,4,3,2,1,0:T(8,128)S(1)}, f32[2,3,1,16,16,128]{5,4,3,2,1,0:T(8,128)S(1)}, f3...) fusion(f32[2,3,6,16,16,128]{5,4,3,2,1,0:T(8,128)} %param.15), kind=kLoop, calls=%fused_computation.187 | loop fusion | bytes 9437184 | tf_op jit(solution)/shard_map/slice | solution.py:66
  20.8 3.6 %copy.120 = f32[2,3,6,16,16,128]{5,3,0,1,4,2:T(8,128)} copy(f32[2,3,6,16,16,128]{5,4,3,2,1,0:T(8,128)S(1)} %bitcast.212) | data formatting | bytes 9437184 | tf_op args[0]
  25.2 2.0 %fusion.49 = (f32[2,1,6,16,16,128]{5,4,3,2,1,0:T(8,128)}, f32[2,1,6,16,16,128]{5,4,3,2,1,0:T(8,128)}) fusion(f32[2,3,6,16,16,128]{5,4,3,2,1,0:T(8,128)S(1)} %bitcast.212), kind=kLoop, calls=%fused_computation.186 | loop fusion | bytes 6291456 | tf_op jit(solution)/shard_map/slice | solution.py:70
  29.1 1.0 slice.446
  30.1 0.9 slice.456
  31.0 1.4 %copy_bitcast_fusion.1 = (f32[2,3,16,16,128]{4,2,0,3,1:T(8,128)S(1)}, f32[2,3,16,16,128]{4,2,0,3,1:T(8,128)}) fusion(f32[2,3,1,16,16,128]{5,4,3,2,1,0:T(8,128)S(1)} %get-tuple-element.50, f32[2,3,1,16,16,128]{5,4,3,2,1,0:T(8,128)S(1)} %get-tuple-element.53), kind=kLoop, calls=%fused_computation.50 | loop fusion | bytes 3145728 | tf_op jit(solution)/shard_map/squeeze | solution.py:66
  32.4 1.2 slice.457
  33.8 1.0 slice.443
  35.1 0.9 slice.450
  37.0 1.4 %fusion.52 = (f32[2,1,3,16,16,128]{5,4,3,2,1,0:T(8,128)}, f32[2,1,3,16,16,128]{5,4,3,2,1,0:T(8,128)}, f32[2,1,3,16,16,128]{5,4,3,2,1,0:T(8,128)}) fusion(f32[2,3,3,16,16,128]{5,4,3,2,1,0:T(8,128)S(1)} %copy-done.24), kind=kLoop, calls=%fused_computation.189 | loop fusion | bytes 4718592 | tf_op jit(solution)/shard_map/slice | solution.py:70
  41.4 1.0 copy.154
  42.4 1.0 copy.141
  43.3 1.0 copy.160
  44.3 1.6 %copy.157 = f32[16,16,128]{2,0,1:T(8,128)} copy(f32[16,16,128]{2,1,0:T(8,128)} %broadcast_multiply_fusion) | data formatting | bytes 262144 | tf_op jit(solution)/shard_map/mul | solution.py:110
  45.9 1.6 %copy.156 = f32[16,16,128]{2,0,1:T(8,128)} copy(f32[16,16,128]{2,1,0:T(8,128)} %param.20) | data formatting | bytes 262144 | tf_op args[5]
  49.1 1.6 %copy_bitcast_fusion.8 = (f32[2,3,16,16,128]{4,2,0,3,1:T(8,128)S(1)}, f32[2,3,16,16,128]{4,2,0,3,1:T(8,128)S(1)}) fusion(f32[2,1,3,16,16,128]{5,4,3,2,1,0:T(8,128)S(1)} %copy-done.7, f32[2,1,3,16,16,128]{5,4,3,2,1,0:T(8,128)} %get-tuple-element.75), kind=kLoop, calls=%fused_computation.65 | loop fusion | bytes 3145728 | tf_op jit(solution)/shard_map/squeeze | solution.py:70
  50.8 1.4 %pad_maximum_fusion.4 = (f32[2,3,6,18,1,128]{5,3,0,1,4,2:T(8,128)S(1)}, f32[2,3,6,18,1,128]{5,3,0,1,4,2:T(8,128)S(1)}) fusion(f32[2,3,6,1,16,128]{5,3,0,1,4,2:T(1,128)} %collective-permute-done, f32[2,3,6,16,16,128]{5,3,0,1,4,2:T(8,128)} %copy.120, f32[2,3,6,1,16,128]{5,3,0,1,4,2:T(1,128)} %collective-permute-done.1), kind=kLoop, calls=%fused_computation.72 | loop fusion | flops 331776 | bytes 5971968 | tf_op jit(solution)/shard_map/concatenate | solution.py:26
  52.1 1.3 %collective-permute-start.3 = (f32[2,3,6,18,1,128]{5,3,0,1,4,2:T(8,128)S(1)}, f32[2,3,6,18,1,128]{5,3,0,1,4,2:T(8,128)S(1)}, u32[]{:S(2)}, u32[]{:S(2)}) collective-permute-start(f32[2,3,6,18,1,128]{5,3,0,1,4,2:T(8,128)S(1)} %get-tuple-element.42), channel_id=1, source_target_pairs={{1,0},{2,1},{3,2},{5,4},{6,5},{7,6},{9,8},{10,9},{11,10},{13,12},{... | collective-permute-start | bytes 995336 | tf_op jit(solution)/shard_map/ppermute | solution.py:30
  53.5 4.8 %collective-permute-start.2 = (f32[2,3,6,18,1,128]{5,3,0,1,4,2:T(8,128)S(1)}, f32[2,3,6,18,1,128]{5,3,0,1,4,2:T(8,128)S(1)}, u32[]{:S(2)}, u32[]{:S(2)}) collective-permute-start(f32[2,3,6,18,1,128]{5,3,0,1,4,2:T(8,128)S(1)} %get-tuple-element.43), channel_id=1, source_target_pairs={{0,1},{1,2},{2,3},{4,5},{5,6},{6,7},{8,9},{9,10},{10,11},{12,13},{... | collective-permute-start | bytes 995336 | tf_op jit(solution)/shard_map/ppermute | solution.py:28
  58.3 0.8 fusion.53
  59.2 0.8 slice.444
  60.1 5.6 %collective-permute-done.3 = f32[2,3,6,18,1,128]{5,3,0,1,4,2:T(8,128)S(1)} collective-permute-done((f32[2,3,6,18,1,128]{5,3,0,1,4,2:T(8,128)S(1)}, f32[2,3,6,18,1,128]{5,3,0,1,4,2:T(8,128)S(1)}, u32[]{:S(2)}, u32[]{:S(2)}) %collective-permute-start.3) | collective-permute-done | bytes 331808 | tf_op jit(solution)/shard_map/ppermute | solution.py:30
  65.9 1.0 fusion.7
  68.1 2.0 %fusion.4 = (f32[2,3,1,16,16,128]{5,3,0,4,2,1:T(8,128)S(1)}, f32[2,3,1,16,16,128]{5,3,0,4,2,1:T(8,128)S(1)}) fusion(f32[2,3,1,16,128]{4,2,0,3,1:T(1,128)S(1)} %copy.117, f32[2,3,15,16,128]{4,2,0,3,1:T(8,128)S(1)} %copy-done.20, f32[2,3,16,15,128]{4,2,0,3,1:T(8,128)S(1)} %copy-done.21, f32[2,3,16,1,128]{4,2,0,3,1:T(8,128)S(1)} %get-tuple-element.80, ...), kind=kLoop, calls=%fused_computation.18 | loop fusion | flops 2752512 | bytes 10211328 | tf_op jit(solution)/shard_map/stack | solution.py:89
  70.4 1.0 copy-done.8
  75.0 3.8 %collective-permute-start.4 = (f32[2,3,3,1,16,128]{5,3,0,1,4,2:T(1,128)S(1)}, f32[2,3,3,1,16,128]{5,3,0,1,4,2:T(1,128)S(1)}, u32[]{:S(2)}, u32[]{:S(2)}) collective-permute-start(f32[2,3,3,1,16,128]{5,3,0,1,4,2:T(1,128)S(1)} %get-tuple-element.70), channel_id=1, source_target_pairs={{0,4},{4,8},{8,12},{1,5},{5,9},{9,13},{2,6},{6,10},{10,14},{3,7},{... | collective-permute-start | bytes 442376 | tf_op jit(solution)/shard_map/ppermute | solution.py:28
  78.7 1.3 %collective-permute-start.5 = (f32[2,3,3,1,16,128]{5,3,0,1,4,2:T(1,128)S(1)}, f32[2,3,3,1,16,128]{5,3,0,1,4,2:T(1,128)S(1)}, u32[]{:S(2)}, u32[]{:S(2)}) collective-permute-start(f32[2,3,3,1,16,128]{5,3,0,1,4,2:T(1,128)S(1)} %get-tuple-element.69), channel_id=1, source_target_pairs={{4,0},{8,4},{12,8},{5,1},{9,5},{13,9},{6,2},{10,6},{14,10},{7,3},{... | collective-permute-start | bytes 442376 | tf_op jit(solution)/shard_map/ppermute | solution.py:30
  80.0 2.1 %copy.162 = f32[2,2,3,16,16,128]{5,4,3,2,1,0:T(8,128)} copy(f32[2,2,3,16,16,128]{5,3,0,1,4,2:T(8,128)S(1)} %pad_maximum_fusion.3) | data formatting | bytes 3145728
  82.1 3.9 %collective-permute-done.5 = f32[2,3,3,1,16,128]{5,3,0,1,4,2:T(1,128)S(1)} collective-permute-done((f32[2,3,3,1,16,128]{5,3,0,1,4,2:T(1,128)S(1)}, f32[2,3,3,1,16,128]{5,3,0,1,4,2:T(1,128)S(1)}, u32[]{:S(2)}, u32[]{:S(2)}) %collective-permute-start.5) | collective-permute-done | bytes 147488 | tf_op jit(solution)/shard_map/ppermute | solution.py:30
  86.1 1.3 %collective-permute-start.7 = (f32[2,3,3,18,1,128]{5,3,0,1,4,2:T(8,128)S(1)}, f32[2,3,3,18,1,128]{5,3,0,1,4,2:T(8,128)S(1)}, u32[]{:S(2)}, u32[]{:S(2)}) collective-permute-start(f32[2,3,3,18,1,128]{5,3,0,1,4,2:T(8,128)S(1)} %get-tuple-element.58), channel_id=1, source_target_pairs={{1,0},{2,1},{3,2},{5,4},{6,5},{7,6},{9,8},{10,9},{11,10},{13,12},{... | collective-permute-start | bytes 497672 | tf_op jit(solution)/shard_map/ppermute | solution.py:30
  87.4 4.8 %collective-permute-start.6 = (f32[2,3,3,18,1,128]{5,3,0,1,4,2:T(8,128)S(1)}, f32[2,3,3,18,1,128]{5,3,0,1,4,2:T(8,128)S(1)}, u32[]{:S(2)}, u32[]{:S(2)}) collective-permute-start(f32[2,3,3,18,1,128]{5,3,0,1,4,2:T(8,128)S(1)} %get-tuple-element.59), channel_id=1, source_target_pairs={{0,1},{1,2},{2,3},{4,5},{5,6},{6,7},{8,9},{9,10},{10,11},{12,13},{... | collective-permute-start | bytes 497672 | tf_op jit(solution)/shard_map/ppermute | solution.py:28
  92.2 1.7 %collective-permute-done.7 = f32[2,3,3,18,1,128]{5,3,0,1,4,2:T(8,128)S(1)} collective-permute-done((f32[2,3,3,18,1,128]{5,3,0,1,4,2:T(8,128)S(1)}, f32[2,3,3,18,1,128]{5,3,0,1,4,2:T(8,128)S(1)}, u32[]{:S(2)}, u32[]{:S(2)}) %collective-permute-start.7) | collective-permute-done | bytes 165920 | tf_op jit(solution)/shard_map/ppermute | solution.py:30
  93.9 1.4 %collective-permute-done.6 = f32[2,3,3,18,1,128]{5,3,0,1,4,2:T(8,128)S(1)} collective-permute-done((f32[2,3,3,18,1,128]{5,3,0,1,4,2:T(8,128)S(1)}, f32[2,3,3,18,1,128]{5,3,0,1,4,2:T(8,128)S(1)}, u32[]{:S(2)}, u32[]{:S(2)}) %collective-permute-start.6) | collective-permute-done | bytes 165920 | tf_op jit(solution)/shard_map/ppermute | solution.py:28
  95.4 0.9 slice_bitcast_fusion.17
  97.8 1.7 %slice_bitcast_fusion.1 = (f32[2,6,16,16,128]{4,2,0,3,1:T(8,128)S(1)}, f32[2,6,16,16,128]{4,2,0,3,1:T(8,128)S(1)}, f32[2,6,16,16,128]{4,2,0,3,1:T(8,128)}) fusion(f32[2,3,6,16,16,128]{5,3,0,4,2,1:T(8,128)S(1)} %fusion.16), kind=kLoop, calls=%fused_computation.4 | loop fusion | bytes 9437184 | tf_op jit(solution)/shard_map/squeeze | solution.py:70
  100.3 0.8 copy-done
  101.7 1.1 add_multiply_fusion
  103.0 0.9 copy.232
  104.0 1.1 bitcast_dynamic-update-slice_fusion.12
  105.1 1.2 bitcast_dynamic-update-slice_fusion.11
  107.8 1.2 copy-done.1
  111.5 3.5 %copy.163 = f32[2,2,6,16,16,128]{5,4,3,2,1,0:T(8,128)} copy(f32[2,2,6,16,16,128]{5,3,0,4,2,1:T(8,128)S(1)} %pad_maximum_fusion) | data formatting | bytes 6291456
  115.0 1.0 copy.182
  (172 shorter events, 21.7 us)
Async XLA Ops:
  7.2 107.9 %reduce-scatter.5.cloned.1.call-start = ((), (), s32[]{:S(2)}) async-start(), calls=%async_computation.1 | async-start | bytes 589824
  9.3 41.4 %collective-permute-start = (f32[2,3,6,1,16,128]{5,3,0,1,4,2:T(1,128)}, f32[2,3,6,1,16,128]{5,3,0,1,4,2:T(1,128)}, u32[]{:S(2)}, u32[]{:S(2)}) collective-permute-start(f32[2,3,6,1,16,128]{5,3,0,1,4,2:T(1,128)} %copy.116), channel_id=1, source_target_pairs={{4,0},{8,4},{12,8},{5,1},{9,5},{13,9},{6,2},{10,6},{14,10},{7,3},{... | collective-permute-start | bytes 884744 | tf_op jit(solution)/shard_map/ppermute | solution.py:30
  10.6 10.1 %slice-start = ((s8[4718592]{0:T(1024)(128)(4,1)}), s8[4194304]{0:T(1024)(128)(4,1)S(1)}, s32[]{:S(2)}) async-start(s8[4718592]{0:T(1024)(128)(4,1)} %bitcast.211), calls=%async_computation.2 | async-start | bytes 8388608
  11.7 9.1 %slice-start.1 = ((s8[4718592]{0:T(1024)(128)(4,1)}), s8[524288]{0:T(1024)(128)(4,1)S(1)}, s32[]{:S(2)}) async-start(s8[4718592]{0:T(1024)(128)(4,1)} %bitcast.211), calls=%async_computation.3 | async-start | bytes 1048576
  11.7 39.1 %collective-permute-start.1 = (f32[2,3,6,1,16,128]{5,3,0,1,4,2:T(1,128)}, f32[2,3,6,1,16,128]{5,3,0,1,4,2:T(1,128)}, u32[]{:S(2)}, u32[]{:S(2)}) collective-permute-start(f32[2,3,6,1,16,128]{5,3,0,1,4,2:T(1,128)} %copy.119), channel_id=1, source_target_pairs={{0,4},{4,8},{8,12},{1,5},{5,9},{9,13},{2,6},{6,10},{10,14},{3,7},{... | collective-permute-start | bytes 884744 | tf_op jit(solution)/shard_map/ppermute | solution.py:28
  20.8 10.3 %copy-start.5 = (f32[2,3,1,16,16,128]{5,4,3,2,1,0:T(8,128)}, f32[2,3,1,16,16,128]{5,4,3,2,1,0:T(8,128)S(1)}, u32[]{:S(2)}) copy-start(f32[2,3,1,16,16,128]{5,4,3,2,1,0:T(8,128)S(1)} %get-tuple-element.53) | copy-start | bytes 2359300
  20.8 14.0 %copy-start.10 = (f32[2,3,1,16,16,128]{5,4,3,2,1,0:T(8,128)}, f32[2,3,1,16,16,128]{5,4,3,2,1,0:T(8,128)S(1)}, u32[]{:S(2)}) copy-start(f32[2,3,1,16,16,128]{5,4,3,2,1,0:T(8,128)S(1)} %get-tuple-element.52) | copy-start | bytes 2359300
  20.8 3.6 %copy-start.31 = (f32[16,16,128]{2,1,0:T(8,128)S(1)}, f32[16,16,128]{2,1,0:T(8,128)}, u32[]{:S(2)}) copy-start(f32[16,16,128]{2,1,0:T(8,128)} %param.18) | copy-start | bytes 393220
  25.2 2.0 %copy-start.32 = (f32[16,16,128]{2,1,0:T(8,128)S(1)}, f32[16,16,128]{2,1,0:T(8,128)}, u32[]{:S(2)}) copy-start(f32[16,16,128]{2,1,0:T(8,128)} %param.21) | copy-start | bytes 393220
  29.0 3.4 %copy-start.12 = (f32[2,3,16,16,128]{4,2,0,3,1:T(8,128)}, f32[2,3,16,16,128]{4,2,0,3,1:T(8,128)S(1)}, u32[]{:S(2)}) copy-start(f32[2,3,16,16,128]{4,2,0,3,1:T(8,128)S(1)} %get-tuple-element.102) | copy-start | bytes 2359300
  29.0 3.4 %copy-start.14 = (f32[2,3,16,16,128]{4,2,0,3,1:T(8,128)}, f32[2,3,16,16,128]{4,2,0,3,1:T(8,128)S(1)}, u32[]{:S(2)}) copy-start(f32[2,3,16,16,128]{4,2,0,3,1:T(8,128)S(1)} %get-tuple-element.103) | copy-start | bytes 2359300
  34.8 1.2 copy-start.33
  34.8 1.2 copy-start.34
  35.0 2.0 %copy-start.24 = (f32[2,3,3,16,16,128]{5,4,3,2,1,0:T(8,128)S(1)}, f32[2,3,3,16,16,128]{5,4,3,2,1,0:T(8,128)}, u32[]{:S(2)}) copy-start(f32[2,3,3,16,16,128]{5,4,3,2,1,0:T(8,128)} %param.16) | copy-start | bytes 7077892
  37.0 2.1 %copy-start.38 = (s32[2]{0:T(128)S(1)}, s32[2]{0:T(128)}, u32[]{:S(2)}) copy-start(s32[2]{0:T(128)} %param.23) | copy-start | bytes 28
  37.0 3.3 %copy-start.35 = (s32[2,512]{1,0:T(2,128)S(1)}, s32[2,512]{1,0:T(2,128)}, u32[]{:S(2)}) copy-start(s32[2,512]{1,0:T(2,128)} %param.25) | copy-start | bytes 12292
  40.4 0.9 copy-start.36
  41.4 7.7 %copy-start.7 = (f32[2,1,3,16,16,128]{5,4,3,2,1,0:T(8,128)S(1)}, f32[2,1,3,16,16,128]{5,4,3,2,1,0:T(8,128)}, u32[]{:S(2)}) copy-start(f32[2,1,3,16,16,128]{5,4,3,2,1,0:T(8,128)} %get-tuple-element.73) | copy-start | bytes 2359300
  43.3 56.2 %copy-start.28 = (f32[16,16,128]{2,0,1:T(8,128)}, f32[16,16,128]{2,0,1:T(8,128)S(1)}, u32[]{:S(2)}) copy-start(f32[16,16,128]{2,0,1:T(8,128)S(1)} %copy.141) | copy-start | bytes 393220
  50.7 15.1 %copy-start.11 = (f32[2,3,1,16,16,128]{5,4,3,2,1,0:T(8,128)S(1)}, f32[2,3,1,16,16,128]{5,4,3,2,1,0:T(8,128)}, u32[]{:S(2)}) copy-start(f32[2,3,1,16,16,128]{5,4,3,2,1,0:T(8,128)} %copy-done.10) | copy-start | bytes 2359300
  50.7 15.1 %copy-start.13 = (f32[2,3,16,16,128]{4,2,0,3,1:T(8,128)S(1)}, f32[2,3,16,16,128]{4,2,0,3,1:T(8,128)}, u32[]{:S(2)}) copy-start(f32[2,3,16,16,128]{4,2,0,3,1:T(8,128)} %copy-done.12) | copy-start | bytes 2359300
  50.7 15.1 %copy-start.15 = (f32[2,3,16,16,128]{4,2,0,3,1:T(8,128)S(1)}, f32[2,3,16,16,128]{4,2,0,3,1:T(8,128)}, u32[]{:S(2)}) copy-start(f32[2,3,16,16,128]{4,2,0,3,1:T(8,128)} %copy-done.14) | copy-start | bytes 2359300
  50.7 15.1 %copy-start.23 = (f32[2,3,16,15,128]{4,2,0,3,1:T(8,128)S(1)}, f32[2,3,16,15,128]{4,2,0,3,1:T(8,128)}, u32[]{:S(2)}) copy-start(f32[2,3,16,15,128]{4,2,0,3,1:T(8,128)} %slice.450) | copy-start | bytes 2211844
  52.1 13.6 %collective-permute-start.3 = (f32[2,3,6,18,1,128]{5,3,0,1,4,2:T(8,128)S(1)}, f32[2,3,6,18,1,128]{5,3,0,1,4,2:T(8,128)S(1)}, u32[]{:S(2)}, u32[]{:S(2)}) collective-permute-start(f32[2,3,6,18,1,128]{5,3,0,1,4,2:T(8,128)S(1)} %get-tuple-element.42), channel_id=1, source_target_pairs={{1,0},{2,1},{3,2},{5,4},{6,5},{7,6},{9,8},{10,9},{11,10},{13,12},{... | collective-permute-start | bytes 995336 | tf_op jit(solution)/shard_map/ppermute | solution.py:30
  53.5 13.5 %collective-permute-start.2 = (f32[2,3,6,18,1,128]{5,3,0,1,4,2:T(8,128)S(1)}, f32[2,3,6,18,1,128]{5,3,0,1,4,2:T(8,128)S(1)}, u32[]{:S(2)}, u32[]{:S(2)}) collective-permute-start(f32[2,3,6,18,1,128]{5,3,0,1,4,2:T(8,128)S(1)} %get-tuple-element.43), channel_id=1, source_target_pairs={{0,1},{1,2},{2,3},{4,5},{5,6},{6,7},{8,9},{9,10},{10,11},{12,13},{... | collective-permute-start | bytes 995336 | tf_op jit(solution)/shard_map/ppermute | solution.py:28
  65.8 1.2 copy-start.6
  65.8 1.4 %copy-start.9 = (f32[2,3,16,16,128]{4,2,0,3,1:T(8,128)S(1)}, f32[2,3,16,16,128]{4,2,0,3,1:T(8,128)}, u32[]{:S(2)}) copy-start(f32[2,3,16,16,128]{4,2,0,3,1:T(8,128)} %get-tuple-element.101) | copy-start | bytes 2359300
  65.8 1.6 %copy-start.19 = (f32[2,3,16,16,127]{4,2,0,3,1:T(8,128)S(1)}, f32[2,3,16,16,127]{4,2,0,3,1:T(8,128)}, u32[]{:S(2)}) copy-start(f32[2,3,16,16,127]{4,2,0,3,1:T(8,128)} %slice.457) | copy-start | bytes 2340868
  65.8 1.8 %copy-start.20 = (f32[2,3,15,16,128]{4,2,0,3,1:T(8,128)S(1)}, f32[2,3,15,16,128]{4,2,0,3,1:T(8,128)}, u32[]{:S(2)}) copy-start(f32[2,3,15,16,128]{4,2,0,3,1:T(8,128)} %slice.443) | copy-start | bytes 2211844
  65.8 2.0 %copy-start.21 = (f32[2,3,16,15,128]{4,2,0,3,1:T(8,128)S(1)}, f32[2,3,16,15,128]{4,2,0,3,1:T(8,128)}, u32[]{:S(2)}) copy-start(f32[2,3,16,15,128]{4,2,0,3,1:T(8,128)} %slice.446) | copy-start | bytes 2211844
  65.8 2.2 %copy-start.22 = (f32[2,3,16,15,128]{4,2,0,3,1:T(8,128)S(1)}, f32[2,3,16,15,128]{4,2,0,3,1:T(8,128)}, u32[]{:S(2)}) copy-start(f32[2,3,16,15,128]{4,2,0,3,1:T(8,128)} %slice.456) | copy-start | bytes 2211844
  70.3 1.1 copy-start.8
  70.3 1.1 copy-start.30
  71.4 1.1 copy-start.18
  75.0 7.2 %collective-permute-start.4 = (f32[2,3,3,1,16,128]{5,3,0,1,4,2:T(1,128)S(1)}, f32[2,3,3,1,16,128]{5,3,0,1,4,2:T(1,128)S(1)}, u32[]{:S(2)}, u32[]{:S(2)}) collective-permute-start(f32[2,3,3,1,16,128]{5,3,0,1,4,2:T(1,128)S(1)} %get-tuple-element.70), channel_id=1, source_target_pairs={{0,4},{4,8},{8,12},{1,5},{5,9},{9,13},{2,6},{6,10},{10,14},{3,7},{... | collective-permute-start | bytes 442376 | tf_op jit(solution)/shard_map/ppermute | solution.py:28
  78.7 7.3 %collective-permute-start.5 = (f32[2,3,3,1,16,128]{5,3,0,1,4,2:T(1,128)S(1)}, f32[2,3,3,1,16,128]{5,3,0,1,4,2:T(1,128)S(1)}, u32[]{:S(2)}, u32[]{:S(2)}) collective-permute-start(f32[2,3,3,1,16,128]{5,3,0,1,4,2:T(1,128)S(1)} %get-tuple-element.69), channel_id=1, source_target_pairs={{4,0},{8,4},{12,8},{5,1},{9,5},{13,9},{6,2},{10,6},{14,10},{7,3},{... | collective-permute-start | bytes 442376 | tf_op jit(solution)/shard_map/ppermute | solution.py:30
  86.1 7.8 %collective-permute-start.7 = (f32[2,3,3,18,1,128]{5,3,0,1,4,2:T(8,128)S(1)}, f32[2,3,3,18,1,128]{5,3,0,1,4,2:T(8,128)S(1)}, u32[]{:S(2)}, u32[]{:S(2)}) collective-permute-start(f32[2,3,3,18,1,128]{5,3,0,1,4,2:T(8,128)S(1)} %get-tuple-element.58), channel_id=1, source_target_pairs={{1,0},{2,1},{3,2},{5,4},{6,5},{7,6},{9,8},{10,9},{11,10},{13,12},{... | collective-permute-start | bytes 497672 | tf_op jit(solution)/shard_map/ppermute | solution.py:30
  87.4 8.0 %collective-permute-start.6 = (f32[2,3,3,18,1,128]{5,3,0,1,4,2:T(8,128)S(1)}, f32[2,3,3,18,1,128]{5,3,0,1,4,2:T(8,128)S(1)}, u32[]{:S(2)}, u32[]{:S(2)}) collective-permute-start(f32[2,3,3,18,1,128]{5,3,0,1,4,2:T(8,128)S(1)} %get-tuple-element.59), channel_id=1, source_target_pairs={{0,1},{1,2},{2,3},{4,5},{5,6},{6,7},{8,9},{9,10},{10,11},{12,13},{... | collective-permute-start | bytes 497672 | tf_op jit(solution)/shard_map/ppermute | solution.py:28
  99.7 1.5 %copy-start = (f32[2,1,6,16,16,128]{5,4,3,2,1,0:T(8,128)S(1)}, f32[2,1,6,16,16,128]{5,4,3,2,1,0:T(8,128)}, u32[]{:S(2)}) copy-start(f32[2,1,6,16,16,128]{5,4,3,2,1,0:T(8,128)} %get-tuple-element.48) | copy-start | bytes 4718596
  102.8 1.1 copy-start.26
  103.9 2.3 %copy-start.17 = (f32[2,1,16,16,128]{4,2,0,3,1:T(8,128)S(1)}, f32[2,1,16,16,128]{4,2,0,3,1:T(8,128)}, u32[]{:S(2)}) copy-start(f32[2,1,16,16,128]{4,2,0,3,1:T(8,128)} %get-tuple-element.37) | copy-start | bytes 786436
  103.9 2.3 %copy-start.27 = (f32[16,16,128]{2,0,1:T(8,128)S(1)}, f32[16,16,128]{2,0,1:T(8,128)}, u32[]{:S(2)}) copy-start(f32[16,16,128]{2,0,1:T(8,128)} %copy.156) | copy-start | bytes 393220
  103.9 2.4 %copy-start.25 = (f32[16,16,128]{2,0,1:T(8,128)S(1)}, f32[16,16,128]{2,0,1:T(8,128)}, u32[]{:S(2)}) copy-start(f32[16,16,128]{2,0,1:T(8,128)} %copy.158) | copy-start | bytes 393220
  105.0 1.6 %copy-start.4 = (f32[2,6,16,16,128]{4,2,0,3,1:T(8,128)S(1)}, f32[2,6,16,16,128]{4,2,0,3,1:T(8,128)}, u32[]{:S(2)}) copy-start(f32[2,6,16,16,128]{4,2,0,3,1:T(8,128)} %get-tuple-element.46) | copy-start | bytes 4718596
  105.1 1.6 %copy-start.29 = (f32[16,16,128]{2,0,1:T(8,128)S(1)}, f32[16,16,128]{2,0,1:T(8,128)}, u32[]{:S(2)}) copy-start(f32[16,16,128]{2,0,1:T(8,128)} %copy-done.28) | copy-start | bytes 393220
  106.4 1.0 copy-start.3
  107.6 1.4 %copy-start.1 = (f32[2,1,6,16,16,128]{5,4,3,2,1,0:T(8,128)S(1)}, f32[2,1,6,16,16,128]{5,4,3,2,1,0:T(8,128)}, u32[]{:S(2)}) copy-start(f32[2,1,6,16,16,128]{5,4,3,2,1,0:T(8,128)} %get-tuple-element.48) | copy-start | bytes 4718596
  109.1 1.4 %copy-start.16 = (f32[2,1,6,16,16,128]{5,4,3,2,1,0:T(8,128)S(1)}, f32[2,1,6,16,16,128]{5,4,3,2,1,0:T(8,128)}, u32[]{:S(2)}) copy-start(f32[2,1,6,16,16,128]{5,4,3,2,1,0:T(8,128)} %get-tuple-element.47) | copy-start | bytes 4718596
  (2 other events, 1.4 us)
Sparse Core Ops, SparseCore 0:
  104.0 9.4 reduce-scatter.4
where the time goes:
time: 124 us
  local copies, waits for them, and re-layouts  49.3 us (40%)
  starting transfers between devices  24.9 us (20%)
  other arithmetic  21.5 us (17%)
  between operations  14.9 us (12%)
  waiting for transfers between devices  12.7 us (10%)
    unnamed x98, local copies, waits for them, and re-layouts  22.2 us
    ppermute x4, starting transfers between devices, extended(): lax.ppermute(tail, axis, [(i, (i + 1) % count) for i in range(ends)])  19.7 us
    ppermute x4, waiting for transfers between devices, extended(): lax.ppermute(head, axis, [((i + 1) % count, i) for i in range(ends)])  11.2 us
    ppermute x4, starting transfers between devices, extended(): lax.ppermute(head, axis, [((i + 1) % count, i) for i in range(ends)])  5.16 us
    slice x2, local copies, waits for them, and re-layouts, wavefield(): return array[..., index, :, :, :, :]  3.46 us
    squeeze x3, local copies, waits for them, and re-layouts, wavefield(): return array[..., index, :, :, :, :]  3.41 us
    unnamed x20, other arithmetic  3.35 us
    another operation x3, other arithmetic, accelerations(): return jnp.stack([accel_x, accel_y, accel_z], axis=-4)  3.19 us
  transfers between devices with their start and end apart: 9, of which 5 were waited for; matrix products, arithmetic and copies ran while one was open for 37% of the time, Pallas kernels for 0%

commit v1 on v0

v1 whole, which is shorter than its diff:
```python
import functools

import jax
import jax.numpy as jnp
from jax import lax
from jax.experimental import pallas as pl
from jax.experimental.pallas import tpu as pltpu
from jax.sharding import PartitionSpec as P

RDEPTH = 2
COURANT = 0.25
MESH = pl.DeviceIdType.MESH


def shifted_up(tile, halo, axis):
    length = tile.shape[axis]
    index = lax.broadcasted_iota(jnp.int32, tile.shape, axis)
    return jnp.where(index == length - 1, halo, pltpu.roll(tile, length - 1, axis))


def shifted_down(tile, halo, axis):
    index = lax.broadcasted_iota(jnp.int32, tile.shape, axis)
    return jnp.where(index == 0, halo, pltpu.roll(tile, 1, axis))


def motion_kernel(
    every_column,
    stress,
    velocity,
    density,
    density_change,
    source_cell,
    source_amp,
    receivers,
    motion_out,
    density_term,
    up_rows,
    low_rows,
    up_cols,
    low_cols,
    st,
    mo,
    record,
    st_up_rows,
    st_low_rows,
    st_up_cols,
    st_low_cols,
    st_up_cols_out,
    st_low_cols_out,
    up_cols_out,
    low_cols_out,
    load_sem,
    store_sem,
    send_sem,
    recv_sem,
):
    shots, waves, _, rows, cols, depth = stress.shape
    gx, gy = lax.axis_index("gx"), lax.axis_index("gy")
    nx, ny = lax.axis_size("gx"), lax.axis_size("gy")
    has_low_x, has_up_x = gx > 0, gx < nx - 1
    has_low_y, has_up_y = gy > 0, gy < ny - 1
    sides = (
        (has_low_x, {"gx": gx - 1}),
        (has_up_x, {"gx": gx + 1}),
        (has_low_y, {"gy": gy - 1}),
        (has_up_y, {"gy": gy + 1}),
    )
    barrier = pltpu.get_barrier_semaphore()
    for present, device in sides:

        @pl.when(present)
        def _(device=device):
            pl.semaphore_signal(barrier, inc=1, device_id=device, device_id_type=MESH)

    loads = []
    for s in range(shots):
        for which, (src, dst) in enumerate(((stress, st), (velocity, mo))):
            copy = pltpu.make_async_copy(src.at[s], dst.at[s], load_sem.at[s, which])
            copy.start()
            loads.append(copy)

    def face(src, dst, slot, device):
        return pltpu.make_async_remote_copy(
            src_ref=src,
            dst_ref=dst,
            send_sem=send_sem.at[slot],
            recv_sem=recv_sem.at[slot],
            device_id=device,
            device_id_type=MESH,
        )

    low_x, up_x, low_y, up_y = (device for _, device in sides)
    stress_rows = (
        (face(stress.at[:, :, 0, 0], st_up_rows, 0, low_x), has_low_x, has_up_x, st_up_rows),
        (
            face(stress.at[:, :, pl.ds(3, 2), rows - 1], st_low_rows, 1, up_x),
            has_up_x,
            has_low_x,
            st_low_rows,
        ),
    )
    stress_cols = [
        (
            (
                face(st_up_cols_out.at[s], st_up_cols.at[s], 2 + 2 * s, low_y),
                has_low_y,
                has_up_y,
                st_up_cols.at[s],
            ),
            (
                face(st_low_cols_out.at[s], st_low_cols.at[s], 3 + 2 * s, up_y),
                has_up_y,
                has_low_y,
                st_low_cols.at[s],
            ),
        )
        for s in range(shots)
    ]
    base = 2 + 2 * shots
    motion_faces = [
        (
            (
                face(mo.at[s, :, pl.ds(1, 2), 0], up_rows.at[s], base + 4 * s, low_x),
                has_low_x,
                has_up_x,
                up_rows.at[s],
            ),
            (
                face(mo.at[s, :, 0, rows - 1], low_rows.at[s], base + 4 * s + 1, up_x),
                has_up_x,
                has_low_x,
                low_rows.at[s],
            ),
            (
                face(up_cols_out.at[s], up_cols.at[s], base + 4 * s + 2, low_y),
                has_low_y,
                has_up_y,
                up_cols.at[s],
            ),
            (
                face(low_cols_out.at[s], low_cols.at[s], base + 4 * s + 3, up_y),
                has_up_y,
                has_low_y,
                low_cols.at[s],
            ),
        )
        for s in range(shots)
    ]

    def send(faces):
        for copy, sends, _, _ in faces:

            @pl.when(sends)
            def _(copy=copy):
                copy.start()

    def receive(faces):
        for copy, _, receives, landing in faces:

            @pl.when(receives)
            def _(copy=copy):
                copy.wait_recv()

            @pl.when(jnp.logical_not(receives))
            def _(landing=landing):
                landing[...] = jnp.zeros(landing.shape, jnp.float32)

    def sent(faces):
        for copy, sends, _, _ in faces:

            @pl.when(sends)
            def _(copy=copy):
                copy.wait_send()

    neighbours = (
        has_low_x.astype(jnp.int32)
        + has_up_x.astype(jnp.int32)
        + has_low_y.astype(jnp.int32)
        + has_up_y.astype(jnp.int32)
    )
    pl.semaphore_wait(barrier, neighbours)
    send(stress_rows)
    row_start, col_start = gx * rows, gy * cols

    for s in range(shots):
        loads[2 * s].wait()
        for w in range(waves):
            st_up_cols_out[s, w] = st[s, w, 1, :, 0, :]
            st_low_cols_out[s, w, 0] = st[s, w, 3, :, cols - 1, :]
            st_low_cols_out[s, w, 1] = st[s, w, 5, :, cols - 1, :]
        send(stress_cols[s])

    count = receivers.shape[1]
    plane = (lax.broadcasted_iota(jnp.int32, (count, depth), 1) == RDEPTH).astype(jnp.bfloat16)
    local = lax.broadcasted_iota(jnp.int32, (rows, cols, count), 0) + row_start
    cell = local * every_column + (
        lax.broadcasted_iota(jnp.int32, (rows, cols, count), 1) + col_start
    )
    cell = cell.reshape(rows * cols, count)
    for s in range(shots):
        marks = jnp.where(receivers[pl.ds(s, 1), :] == cell, 1.0, 0.0).astype(jnp.bfloat16)
        field = jnp.dot(marks, plane, preferred_element_type=jnp.float32)
        record[s] = field.reshape(rows, cols, depth)

    place = (
        lax.broadcasted_iota(jnp.int32, (cols, depth), 0) + col_start
    ) * depth + lax.broadcasted_iota(jnp.int32, (cols, depth), 1)
    receive(stress_rows)
    stores = []
    for s in range(shots):
        loads[2 * s + 1].wait()
        receive(stress_cols[s])
        target, amplitude = source_cell[s], source_amp[s]

        def row(x, carry, s=s, target=target, amplitude=amplitude):
            after = lax.rem(x + 1, rows)
            before = lax.rem(x + rows - 1, rows)
            last, first = x == rows - 1, x == 0
            buoyancy = 1.0 / density[x]
            scaled = COURANT * buoyancy
            change = density_change[x] * buoyancy
            accel = []
            for w in range(waves):
                sxx, syy, szz = st[s, w, 0, x], st[s, w, 1, x], st[s, w, 2, x]
                sxy, sxz, syz = st[s, w, 3, x], st[s, w, 4, x], st[s, w, 5, x]
                sxx_after = jnp.where(last, st_up_rows[s, w], st[s, w, 0, after])
                sxy_before = jnp.where(first, st_low_rows[s, w, 0], st[s, w, 3, before])
                sxz_before = jnp.where(first, st_low_rows[s, w, 1], st[s, w, 4, before])
                syy_halo = st_up_cols[s, w, pl.ds(x, 1), :]
                sxy_halo = st_low_cols[s, w, 0, pl.ds(x, 1), :]
                syz_halo = st_low_cols[s, w, 1, pl.ds(x, 1), :]
                accel.append(
                    (
                        (sxx_after - sxx)
                        + (sxy - shifted_down(sxy, sxy_halo, 0))
                        + (sxz - shifted_down(sxz, 0.0, 1)),
                        (sxy - sxy_before)
                        + (shifted_up(syy, syy_halo, 0) - syy)
                        + (syz - shifted_down(syz, 0.0, 1)),
                        (sxz - sxz_before)
                        + (syz - shifted_down(syz, syz_halo, 0))
                        + (shifted_up(szz, 0.0, 1) - szz),
                    )
                )
            here = place + (x + row_start) * (every_column * depth)
            source = jnp.where(here == target, amplitude, 0.0)
            marks = record[s, x]
            total = None
            for c in range(3):
                first_wave = mo[s, 0, c, x] + scaled * accel[0][c]
                born = mo[s, 1, c, x] + scaled * (accel[1][c] - change * accel[0][c])
                adjoint = mo[s, 2, c, x] + scaled * accel[2][c]
                if c == 2:
                    first_wave = first_wave + scaled * source
                    adjoint = adjoint + scaled * marks * born
                mo[s, 0, c, x] = first_wave
                mo[s, 1, c, x] = born
                mo[s, 2, c, x] = adjoint
                term = accel[0][c] * adjoint
                total = term if total is None else total + term
            total = buoyancy * total
            if s == 0:
                density_term[x] = total
            else:
                density_term[x] = density_term[x] + total
            return carry

        lax.fori_loop(0, rows, row, 0)
        for w in range(waves):
            up_cols_out[s, w, 0] = mo[s, w, 0, :, 0, :]
            up_cols_out[s, w, 1] = mo[s, w, 2, :, 0, :]
            low_cols_out[s, w] = mo[s, w, 1, :, cols - 1, :]
        send(motion_faces[s])
        copy = pltpu.make_async_copy(mo.at[s], motion_out.at[s], store_sem.at[s])
        copy.start()
        stores.append(copy)
    for s in range(shots):
        receive(motion_faces[s])
    sent(stress_rows)
    for s in range(shots):
        sent(stress_cols[s])
        sent(motion_faces[s])
        stores[s].wait()


def stress_kernel(
    stress,
    motion,
    lame,
    shear,
    lame_change,
    shear_change,
    up_rows,
    low_rows,
    up_cols,
    low_cols,
    new_velocity,
    new_stress,
    terms,
):
    _, waves, _, rows, _, _ = motion.shape
    step = pl.program_id(0)

    @pl.when(step == 0)
    def _():
        terms[...] = jnp.zeros(terms.shape, jnp.float32)

    def modulus(strain, first, second, twice):
        trace = first * (strain[0] + strain[1] + strain[2])
        return [trace + twice * strain[i] for i in range(3)] + [
            second * strain[i] for i in range(3, 6)
        ]

    def row(x, carry):
        after = lax.rem(x + 1, rows)
        before = lax.rem(x + rows - 1, rows)
        last, first = x == rows - 1, x == 0
        strain = []
        for w in range(waves):
            vx, vy, vz = motion[0, w, 0, x], motion[0, w, 1, x], motion[0, w, 2, x]
            if w > 0:
                new_velocity[0, w - 1, 0, x] = vx
                new_velocity[0, w - 1, 1, x] = vy
                new_velocity[0, w - 1, 2, x] = vz
            vx_before = jnp.where(first, low_rows[0, w], motion[0, w, 0, before])
            vy_after = jnp.where(last, up_rows[0, w, 0], motion[0, w, 1, after])
            vz_after = jnp.where(last, up_rows[0, w, 1], motion[0, w, 2, after])
            vx_halo = up_cols[0, w, 0, pl.ds(x, 1), :]
            vz_halo = up_cols[0, w, 1, pl.ds(x, 1), :]
            vy_halo = low_cols[0, w, pl.ds(x, 1), :]
            strain.append(
                (
                    vx - vx_before,
                    vy - shifted_down(vy, vy_halo, 0),
                    vz - shifted_down(vz, 0.0, 1),
                    (shifted_up(vx, vx_halo, 0) - vx) + (vy_after - vy),
                    (shifted_up(vx, 0.0, 1) - vx) + (vz_after - vz),
                    (shifted_up(vy, 0.0, 1) - vy) + (shifted_up(vz, vz_halo, 0) - vz),
                )
            )
        first_modulus, second_modulus = lame[x], shear[x]
        twice = 2.0 * second_modulus
        second_change = shear_change[x]
        born = modulus(strain[1], first_modulus, second_modulus, twice)
        changed = modulus(strain[0], lame_change[x], second_change, 2.0 * second_change)
        adjoint = modulus(strain[2], first_modulus, second_modulus, twice)
        a = []
        for c in range(6):
            new_stress[0, 0, c, x] = stress[0, 1, c, x] + COURANT * (born[c] + changed[c])
            value = stress[0, 2, c, x] + COURANT * adjoint[c]
            new_stress[0, 1, c, x] = value
            a.append(value)
        e = strain[0]
        terms[0, x] += (e[0] + e[1] + e[2]) * (a[0] + a[1] + a[2])
        terms[1, x] += (
            2.0 * (e[0] * a[0] + e[1] * a[1] + e[2] * a[2])
            + e[3] * a[3]
            + e[4] * a[4]
            + e[5] * a[5]
        )
        return carry

    lax.fori_loop(0, rows, row, 0)


def share_kernel(
    total_shots, terms, density_term, kernels, landed, landed_density, send_sem, recv_sem
):
    me, count = lax.axis_index("shot"), lax.axis_size("shot")
    rows = kernels.shape[1]
    barrier = pltpu.get_barrier_semaphore()
    for k in range(1, count):
        peer = lax.rem(me + k, count)
        pl.semaphore_signal(barrier, inc=1, device_id={"shot": peer}, device_id_type=MESH)
    pl.semaphore_wait(barrier, count - 1)
    copies = []
    for k in range(1, count):
        peer = lax.rem(me + k, count)
        own = pl.ds(peer * rows, rows)
        for which, (src, dst) in enumerate(
            (
                (terms.at[:, own], landed.at[k - 1]),
                (density_term.at[own], landed_density.at[k - 1]),
            )
        ):
            copy = pltpu.make_async_remote_copy(
                src_ref=src,
                dst_ref=dst,
                send_sem=send_sem.at[k - 1, which],
                recv_sem=recv_sem.at[k - 1, which],
                device_id={"shot": peer},
                device_id_type=MESH,
            )
            copy.start()
            copies.append(copy)
    mine = pl.ds(me * rows, rows)
    total, total_density = terms[:, mine], density_term[mine]
    for k in range(1, count):
        copies[2 * k - 2].wait_recv()
        copies[2 * k - 1].wait_recv()
        total = total + landed[k - 1]
        total_density = total_density + landed_density[k - 1]
    kernels[pl.ds(0, 2)] = total * (1.0 / total_shots)
    kernels[2] = total_density * (1.0 / total_shots)
    for copy in copies:
        copy.wait_send()


def vmem():
    return pl.BlockSpec(memory_space=pltpu.VMEM)


def shards(
    stress_fields,
    velocity_fields,
    lame,
    shear,
    density,
    lame_change,
    shear_change,
    density_change,
    source_cell,
    source_amp,
    receiver_cell,
):
    rows, cols, depth = lame.shape
    shots, waves = stress_fields.shape[:2]
    groups = lax.axis_size("shot")
    every_column = cols * lax.axis_size("gy")
    f32 = jnp.float32
    hbm = pl.BlockSpec(memory_space=pl.ANY)
    smem = pl.BlockSpec(memory_space=pltpu.SMEM)
    transfers = 2 + 6 * shots
    shape = lambda *dims: jax.ShapeDtypeStruct(dims, f32)
    motion, density_term, up_rows, low_rows, up_cols, low_cols = pl.pallas_call(
        functools.partial(motion_kernel, every_column),
        name="motion",
        out_shape=(
            shape(shots, waves, 3, rows, cols, depth),
            shape(rows, cols, depth),
            shape(shots, waves, 2, cols, depth),
            shape(shots, waves, cols, depth),
            shape(shots, waves, 2, rows, depth),
            shape(shots, waves, rows, depth),
        ),
        in_specs=[hbm, hbm, vmem(), vmem(), smem, smem, vmem()],
        out_specs=(hbm, vmem(), vmem(), vmem(), vmem(), vmem()),
        scratch_shapes=[
            pltpu.VMEM((shots, waves, 6, rows, cols, depth), f32),
            pltpu.VMEM((shots, waves, 3, rows, cols, depth), f32),
            pltpu.VMEM((shots, rows, cols, depth), f32),
            pltpu.VMEM((shots, waves, cols, depth), f32),
            pltpu.VMEM((shots, waves, 2, cols, depth), f32),
            pltpu.VMEM((shots, waves, rows, depth), f32),
            pltpu.VMEM((shots, waves, 2, rows, depth), f32),
            pltpu.VMEM((shots, waves, rows, depth), f32),
            pltpu.VMEM((shots, waves, 2, rows, depth), f32),
            pltpu.VMEM((shots, waves, 2, rows, depth), f32),
            pltpu.VMEM((shots, waves, rows, depth), f32),
            pltpu.SemaphoreType.DMA((shots, 2)),
            pltpu.SemaphoreType.DMA((shots,)),
            pltpu.SemaphoreType.DMA((transfers,)),
            pltpu.SemaphoreType.DMA((transfers,)),
        ],
        compiler_params=pltpu.CompilerParams(collective_id=0, has_side_effects=True),
    )(
        stress_fields,
        velocity_fields,
        density,
        density_change,
        source_cell,
        source_amp,
        receiver_cell,
    )

    def per_shot(array):
        rest = array.ndim - 1
        return pl.BlockSpec((1,) + array.shape[1:], lambda s: (s,) + (0,) * rest)

    whole = pl.BlockSpec((rows, cols, depth), lambda s: (0, 0, 0))
    new_velocity, new_stress, terms = pl.pallas_call(
        stress_kernel,
        name="stress",
        grid=(shots,),
        out_shape=(
            shape(shots, 2, 3, rows, cols, depth),
            shape(shots, 2, 6, rows, cols, depth),
            shape(2, rows, cols, depth),
        ),
        in_specs=[
            per_shot(stress_fields),
            per_shot(motion),
            whole,
            whole,
            whole,
            whole,
            per_shot(up_rows),
            per_shot(low_rows),
            per_shot(up_cols),
            per_shot(low_cols),
        ],
        out_specs=(
            pl.BlockSpec((1, 2, 3, rows, cols, depth), lambda s: (s, 0, 0, 0, 0, 0)),
            pl.BlockSpec((1, 2, 6, rows, cols, depth), lambda s: (s, 0, 0, 0, 0, 0)),
            pl.BlockSpec((2, rows, cols, depth), lambda s: (0, 0, 0, 0)),
        ),
    )(
        stress_fields,
        motion,
        lame,
        shear,
        lame_change,
        shear_change,
        up_rows,
        low_rows,
        up_cols,
        low_cols,
    )
    own = rows // groups
    kernels = pl.pallas_call(
        functools.partial(share_kernel, shots * groups),
        name="share",
        out_shape=shape(3, own, cols, depth),
        in_specs=[vmem(), vmem()],
        out_specs=vmem(),
        scratch_shapes=[
            pltpu.VMEM((groups - 1, 2, own, cols, depth), f32),
            pltpu.VMEM((groups - 1, own, cols, depth), f32),
            pltpu.SemaphoreType.DMA((groups - 1, 2)),
            pltpu.SemaphoreType.DMA((groups - 1, 2)),
        ],
        compiler_params=pltpu.CompilerParams(collective_id=1, has_side_effects=True),
    )(terms, density_term)
    return new_velocity, new_stress, kernels


def solution(mesh):
    return jax.shard_map(
        shards,
        mesh=mesh,
        in_specs=(
            P("shot", None, None, "gx", "gy", None),
            P("shot", None, None, "gx", "gy", None),
            P("gx", "gy", None),
            P("gx", "gy", None),
            P("gx", "gy", None),
            P("gx", "gy", None),
            P("gx", "gy", None),
            P("gx", "gy", None),
            P("shot"),
            P("shot"),
            P("shot", None),
        ),
        out_specs=(
            P("shot", None, None, "gx", "gy", None),
            P("shot", None, None, "gx", "gy", None),
            P(None, ("gx", "shot"), "gy", None),
        ),
        check_vma=False,
    )
```

time: 124 us -> 29.2 us (0.24)
  local copies, waits for them, and re-layouts: 49.3 us -> 1.62 us
  Pallas kernels: 0 us -> 26.8 us
  starting transfers between devices: 24.9 us -> 0 us
  other arithmetic: 21.5 us -> 0 us
  between operations: 14.9 us -> 0.65 us
  waiting for transfers between devices: 12.7 us -> 0 us
    pallas_call x0 -> x3, Pallas kernels: none -> 26.8 us  [the longest x1 16.3 us: shards(): pl.pallas_call(functools.partial(motion_kernel, every_column), name='moti...]
    ppermute x8 -> x0, starting transfers between devices: 24.9 us -> none  [the longest x4 19.7 us: extended(): lax.ppermute(tail, axis, [(i, (i + 1) % count) for i in range(ends)])]
    unnamed x98 -> x1, local copies, waits for them, and re-layouts: 22.2 us -> 1.62 us
    slice x20 -> x0, local copies, waits for them, and re-layouts: 16.8 us -> none  [the longest x2 3.46 us: wavefield(): return array[..., index, :, :, :, :]]
    ppermute x8 -> x0, waiting for transfers between devices: 12.7 us -> none  [the longest x4 11.2 us: extended(): lax.ppermute(head, axis, [((i + 1) % count, i) for i in range(ends)])]
    squeeze x6 -> x0, local copies, waits for them, and re-layouts: 5.39 us -> none  [the longest x3 3.41 us: wavefield(): return array[..., index, :, :, :, :]]
    another operation x11 -> x0, other arithmetic: 4.24 us -> none  [the longest x3 3.19 us: accelerations(): return jnp.stack([accel_x, accel_y, accel_z], axis=-4)]
    mul x6 -> x0, other arithmetic: 3.94 us -> none  [the longest x2 1.51 us: point_fields(): source_amp[:, None, None, None] * row_hit[:, :, None, None]]
  transfers between devices with their start and end apart: 9 -> 0, of which waited for: 5 -> 0; matrix products, arithmetic and copies ran while one was open for 37% -> 0% of each run, Pallas kernels for 0% -> 0%
where the time goes in v1:
time: 29.2 us; the launch traced here: 29.1 us
  Pallas kernels  26.8 us (92%)
  local copies, waits for them, and re-layouts  1.62 us (6%)
  between operations  0.65 us (2%)
    pallas_call x1, Pallas kernels, shards(): pl.pallas_call(functools.partial(motion_kernel, every_column), name='moti...  16.3 us
    pallas_call x1, Pallas kernels, shards(): pl.pallas_call(stress_kernel, name='stress', grid=(shots,), out_shape=(sh...  7.34 us
    pallas_call x1, Pallas kernels, shards(): pl.pallas_call(functools.partial(share_kernel, shots * groups), name='sha...  3.16 us
    unnamed x1, local copies, waits for them, and re-layouts  1.62 us

profile of v1, /device:TPU:0, one launch (start us, length us, event | category | flops | bytes accessed | tf_op | source)
XLA Modules:
  0.0 29.1 jit_solution(354404519954420377)
XLA Ops:
  0.6 16.3 %motion.1 = (f32[2,3,3,16,16,128]{5,4,3,2,1,0:T(8,128)}, f32[16,16,128]{2,1,0:T(8,128)}, f32[2,3,2,16,128]{4,3,2,1,0:T(8,128)}, f32[2,3,16,128]{3,2,1,0:T(8,128)...) custom-call(f32[2,3,6,16,16,128]{5,4,3,2,1,0:T(8,128)} %stress.5, f32[2,3,3,16,16,128]{5,4,3,2,1,0:T(8,128)} %velocity.1, ...), custom_call_target="tpu_custom_call" | custom-call | tf_op jit(solution)/shard_map/motion/pallas_call | solution.py:435
  16.9 7.3 %stress.4 = (f32[2,2,3,16,16,128]{5,4,3,2,1,0:T(8,128)}, f32[2,2,6,16,16,128]{5,4,3,2,1,0:T(8,128)}, f32[2,16,16,128]{3,2,1,0:T(8,128)}) custom-call(f32[2,3,6,16,16,128]{5,4,3,2,1,0:T(8,128)} %stress.5, f32[2,3,3,16,16,128]{5,4,3,2,1,0:T(8,128)} %get-tuple-element.12.motion, f32[16,16,128]{2,1,0:T(8,128)} %lame.1, f32[16,16,128]{2,1,0:T(8,128)} %shear.1, ...), custom_call_target="tpu_custom_call" | custom-call | tf_op jit(solution)/shard_map/stress/pallas_call | solution.py:481
  24.3 3.2 %share.1 = f32[3,8,16,128]{3,2,1,0:T(8,128)} custom-call(f32[2,16,16,128]{3,2,1,0:T(8,128)} %get-tuple-element.19.terms, f32[16,16,128]{2,1,0:T(8,128)} %get-tuple-element.20.density_term), custom_call_target="tpu_custom_call" | custom-call | tf_op jit(solution)/shard_map/share/pallas_call | solution.py:520
  27.4 1.6 %copy.15 = f32[3,8,16,128]{3,2,1,0:T(8,128)} copy(f32[3,8,16,128]{3,2,1,0:T(8,128)} %share.1) | data formatting | bytes 393216

commit v2 on v1

v2 whole, which is shorter than its diff:
```python
import functools

import jax
import jax.numpy as jnp
from jax import lax
from jax.experimental import pallas as pl
from jax.experimental.pallas import tpu as pltpu
from jax.sharding import PartitionSpec as P

RDEPTH = 2
COURANT = 0.25
MESH = pl.DeviceIdType.MESH
VMEM_LIMIT = 32 * 1024 * 1024


def shifted_up(tile, halo, axis):
    length = tile.shape[axis]
    index = lax.broadcasted_iota(jnp.int32, tile.shape, axis)
    return jnp.where(index == length - 1, halo, pltpu.roll(tile, length - 1, axis))


def shifted_down(tile, halo, axis):
    index = lax.broadcasted_iota(jnp.int32, tile.shape, axis)
    return jnp.where(index == 0, halo, pltpu.roll(tile, 1, axis))


def step_kernel(
    every_column,
    total_shots,
    stress,
    velocity,
    lame_in,
    shear_in,
    density_in,
    lame_change_in,
    shear_change_in,
    density_change_in,
    receivers_in,
    source_cell,
    source_amp,
    st,
    mo,
    kernels,
    params,
    receivers,
    record,
    accel0,
    strain0,
    terms,
    st_up_rows,
    st_low_rows,
    st_up_cols,
    st_low_cols,
    st_up_cols_out,
    st_low_cols_out,
    up_rows,
    low_rows,
    up_cols,
    low_cols,
    up_cols_out,
    low_cols_out,
    landed,
    load_sem,
    param_sem,
    send_sem,
    recv_sem,
    share_send_sem,
    share_recv_sem,
):
    shots, waves, _, rows, cols, depth = stress.shape
    gx, gy = lax.axis_index("gx"), lax.axis_index("gy")
    nx, ny = lax.axis_size("gx"), lax.axis_size("gy")
    me, groups = lax.axis_index("shot"), lax.axis_size("shot")
    own = rows // groups
    has_low_x, has_up_x = gx > 0, gx < nx - 1
    has_low_y, has_up_y = gy > 0, gy < ny - 1
    sides = (
        (has_low_x, {"gx": gx - 1}),
        (has_up_x, {"gx": gx + 1}),
        (has_low_y, {"gy": gy - 1}),
        (has_up_y, {"gy": gy + 1}),
    )
    barrier = pltpu.get_barrier_semaphore()
    for present, device in sides:

        @pl.when(present)
        def _(device=device):
            pl.semaphore_signal(barrier, inc=1, device_id=device, device_id_type=MESH)

    for k in range(1, groups):
        peer = lax.rem(me + k, groups)
        pl.semaphore_signal(barrier, inc=1, device_id={"shot": peer}, device_id_type=MESH)

    stress_loads = [
        pltpu.make_async_copy(stress.at[s], st.at[s], load_sem.at[s, 0]) for s in range(shots)
    ]
    motion_loads = [
        pltpu.make_async_copy(velocity.at[s], mo.at[s], load_sem.at[s, 1]) for s in range(shots)
    ]
    receiver_load = pltpu.make_async_copy(receivers_in, receivers, param_sem.at[6])
    sources = (density_in, density_change_in, lame_in, shear_in, lame_change_in, shear_change_in)
    param_loads = [
        pltpu.make_async_copy(source, params.at[i], param_sem.at[i])
        for i, source in enumerate(sources)
    ]
    stress_loads[0].start()
    receiver_load.start()
    for copy in stress_loads[1:] + param_loads[:2] + motion_loads + param_loads[2:]:
        copy.start()
    density, density_change, lame, shear, lame_change, shear_change = (
        params.at[i] for i in range(6)
    )

    def face(src, dst, slot, device):
        return pltpu.make_async_remote_copy(
            src_ref=src,
            dst_ref=dst,
            send_sem=send_sem.at[slot],
            recv_sem=recv_sem.at[slot],
            device_id=device,
            device_id_type=MESH,
        )

    low_x, up_x, low_y, up_y = (device for _, device in sides)
    stress_faces, motion_faces = [], []
    for s in range(shots):
        slot = 8 * s
        stress_faces.append(
            (
                (face(stress.at[s, :, 0, 0], st_up_rows.at[s], slot, low_x), has_low_x, has_up_x),
                (
                    face(stress.at[s, :, pl.ds(3, 2), rows - 1], st_low_rows.at[s], slot + 1, up_x),
                    has_up_x,
                    has_low_x,
                ),
                (face(st_up_cols_out.at[s], st_up_cols.at[s], slot + 2, low_y), has_low_y, has_up_y),
                (
                    face(st_low_cols_out.at[s], st_low_cols.at[s], slot + 3, up_y),
                    has_up_y,
                    has_low_y,
                ),
            )
        )
        motion_faces.append(
            (
                (
                    face(mo.at[s, :, pl.ds(1, 2), 0], up_rows.at[s], slot + 4, low_x),
                    has_low_x,
                    has_up_x,
                ),
                (face(mo.at[s, :, 0, rows - 1], low_rows.at[s], slot + 5, up_x), has_up_x, has_low_x),
                (face(up_cols_out.at[s], up_cols.at[s], slot + 6, low_y), has_low_y, has_up_y),
                (face(low_cols_out.at[s], low_cols.at[s], slot + 7, up_y), has_up_y, has_low_y),
            )
        )

    def send(faces):
        for copy, sends, _ in faces:

            @pl.when(sends)
            def _(copy=copy):
                copy.start()

    def sent(faces):
        for copy, sends, _ in faces:

            @pl.when(sends)
            def _(copy=copy):
                copy.wait_send()

    neighbours = groups - 1
    for present, _ in sides:
        neighbours = neighbours + present.astype(jnp.int32)
    pl.semaphore_wait(barrier, neighbours)
    for s in range(shots):
        send(stress_faces[s][:2])
    row_start, col_start = gx * rows, gy * cols

    for s in range(shots):
        stress_loads[s].wait()
        for w in range(waves):
            st_up_cols_out[s, w] = st[s, w, 1, :, 0, :]
            st_low_cols_out[s, w, 0] = st[s, w, 3, :, cols - 1, :]
            st_low_cols_out[s, w, 1] = st[s, w, 5, :, cols - 1, :]
        send(stress_faces[s][2:])

    receiver_load.wait()
    count = receivers.shape[1]
    plane = (lax.broadcasted_iota(jnp.int32, (count, depth), 1) == RDEPTH).astype(jnp.bfloat16)
    cell = (
        lax.broadcasted_iota(jnp.int32, (rows, cols, count), 0) + row_start
    ) * every_column + (lax.broadcasted_iota(jnp.int32, (rows, cols, count), 1) + col_start)
    cell = cell.reshape(rows * cols, count)
    for s in range(shots):
        marks = jnp.where(receivers[pl.ds(s, 1), :] == cell, 1.0, 0.0).astype(jnp.bfloat16)
        field = jnp.dot(marks, plane, preferred_element_type=jnp.float32)
        record[s] = field.reshape(rows, cols, depth)

    place = (
        lax.broadcasted_iota(jnp.int32, (cols, depth), 0) + col_start
    ) * depth + lax.broadcasted_iota(jnp.int32, (cols, depth), 1)
    param_loads[0].wait()
    param_loads[1].wait()

    for s in range(shots):
        motion_loads[s].wait()
        target, amplitude = source_cell[s], source_amp[s]

        def motion_row(x, carry, s=s, target=target, amplitude=amplitude):
            after = lax.rem(x + 1, rows)
            before = lax.rem(x + rows - 1, rows)
            last, first = x == rows - 1, x == 0
            buoyancy = 1.0 / density[x]
            scaled = COURANT * buoyancy
            change = density_change[x] * buoyancy
            accel = []
            for w in range(waves):
                sxx, syy, szz = st[s, w, 0, x], st[s, w, 1, x], st[s, w, 2, x]
                sxy, sxz, syz = st[s, w, 3, x], st[s, w, 4, x], st[s, w, 5, x]
                sxx_after = jnp.where(last, 0.0, st[s, w, 0, after])
                sxy_before = jnp.where(first, 0.0, st[s, w, 3, before])
                sxz_before = jnp.where(first, 0.0, st[s, w, 4, before])
                accel.append(
                    (
                        (sxx_after - sxx)
                        + (sxy - shifted_down(sxy, 0.0, 0))
                        + (sxz - shifted_down(sxz, 0.0, 1)),
                        (sxy - sxy_before)
                        + (shifted_up(syy, 0.0, 0) - syy)
                        + (syz - shifted_down(syz, 0.0, 1)),
                        (sxz - sxz_before)
                        + (syz - shifted_down(syz, 0.0, 0))
                        + (shifted_up(szz, 0.0, 1) - szz),
                    )
                )
            here = place + (x + row_start) * (every_column * depth)
            source = jnp.where(here == target, amplitude, 0.0)
            for c in range(3):
                first_wave = mo[s, 0, c, x] + scaled * accel[0][c]
                born = mo[s, 1, c, x] + scaled * (accel[1][c] - change * accel[0][c])
                adjoint = mo[s, 2, c, x] + scaled * accel[2][c]
                if c == 2:
                    first_wave = first_wave + scaled * source
                    adjoint = adjoint + scaled * record[s, x] * born
                accel0[s, c, x] = accel[0][c]
                mo[s, 0, c, x] = first_wave
                mo[s, 1, c, x] = born
                mo[s, 2, c, x] = adjoint
            return carry

        lax.fori_loop(0, rows, motion_row, 0)

    every = slice(None)
    low_face, up_face = (0, every), (rows - 1, every)
    left_face, right_face = (every, 0), (every, cols - 1)

    def fix_motion(s, where, c, halo, sign):
        at = where + (every,)
        buoyancy = 1.0 / density[at]
        scaled = COURANT * buoyancy
        change = density_change[at] * buoyancy
        d0, d1, d2 = (sign * halo[w] for w in range(waves))
        accel0[(s, c) + at] += d0
        mo[(s, 0, c) + at] += scaled * d0
        born = scaled * (d1 - change * d0)
        mo[(s, 1, c) + at] += born
        adjoint = scaled * d2
        if c == 2:
            adjoint = adjoint + scaled * record[(s,) + at] * born
        mo[(s, 2, c) + at] += adjoint

    def layers(ref, s, which=None):
        if which is None:
            return [ref[s, w] for w in range(waves)]
        return [ref[s, w, which] for w in range(waves)]

    for s in range(shots):
        (up_x_copy, _, up_x_in), (low_x_copy, _, low_x_in), (up_y_copy, _, up_y_in), (
            low_y_copy,
            _,
            low_y_in,
        ) = stress_faces[s]

        @pl.when(up_x_in)
        def _(s=s, copy=up_x_copy):
            copy.wait_recv()
            fix_motion(s, up_face, 0, layers(st_up_rows, s), 1.0)

        @pl.when(low_x_in)
        def _(s=s, copy=low_x_copy):
            copy.wait_recv()
            fix_motion(s, low_face, 1, layers(st_low_rows, s, 0), -1.0)
            fix_motion(s, low_face, 2, layers(st_low_rows, s, 1), -1.0)

        @pl.when(up_y_in)
        def _(s=s, copy=up_y_copy):
            copy.wait_recv()
            fix_motion(s, right_face, 1, layers(st_up_cols, s), 1.0)

        @pl.when(low_y_in)
        def _(s=s, copy=low_y_copy):
            copy.wait_recv()
            fix_motion(s, left_face, 0, layers(st_low_cols, s, 0), -1.0)
            fix_motion(s, left_face, 2, layers(st_low_cols, s, 1), -1.0)

        send(motion_faces[s][:2])
        for w in range(waves):
            up_cols_out[s, w, 0] = mo[s, w, 0, :, 0, :]
            up_cols_out[s, w, 1] = mo[s, w, 2, :, 0, :]
            low_cols_out[s, w] = mo[s, w, 1, :, cols - 1, :]
        send(motion_faces[s][2:])

    for copy in param_loads[2:]:
        copy.wait()

    def modulus(strain, first, second, twice):
        trace = first * (strain[0] + strain[1] + strain[2])
        return [trace + twice * strain[i] for i in range(3)] + [
            second * strain[i] for i in range(3, 6)
        ]

    for s in range(shots):

        def stress_row(x, carry, s=s):
            after = lax.rem(x + 1, rows)
            before = lax.rem(x + rows - 1, rows)
            last, first = x == rows - 1, x == 0
            strain, adjoint_motion = [], None
            for w in range(waves):
                vx, vy, vz = mo[s, w, 0, x], mo[s, w, 1, x], mo[s, w, 2, x]
                adjoint_motion = (vx, vy, vz)
                vx_before = jnp.where(first, 0.0, mo[s, w, 0, before])
                vy_after = jnp.where(last, 0.0, mo[s, w, 1, after])
                vz_after = jnp.where(last, 0.0, mo[s, w, 2, after])
                strain.append(
                    (
                        vx - vx_before,
                        vy - shifted_down(vy, 0.0, 0),
                        vz - shifted_down(vz, 0.0, 1),
                        (shifted_up(vx, 0.0, 0) - vx) + (vy_after - vy),
                        (shifted_up(vx, 0.0, 1) - vx) + (vz_after - vz),
                        (shifted_up(vy, 0.0, 1) - vy) + (shifted_up(vz, 0.0, 0) - vz),
                    )
                )
            first_modulus, second_modulus = lame[x], shear[x]
            twice = 2.0 * second_modulus
            second_change = shear_change[x]
            born = modulus(strain[1], first_modulus, second_modulus, twice)
            changed = modulus(strain[0], lame_change[x], second_change, 2.0 * second_change)
            adjoint = modulus(strain[2], first_modulus, second_modulus, twice)
            for c in range(6):
                strain0[s, c, x] = strain[0][c]
                st[s, 1, c, x] = st[s, 1, c, x] + COURANT * (born[c] + changed[c])
                st[s, 2, c, x] = st[s, 2, c, x] + COURANT * adjoint[c]
            total = (
                accel0[s, 0, x] * adjoint_motion[0]
                + accel0[s, 1, x] * adjoint_motion[1]
                + accel0[s, 2, x] * adjoint_motion[2]
            )
            total = (1.0 / density[x]) * total
            terms[2, x] = total if s == 0 else terms[2, x] + total
            return carry

        lax.fori_loop(0, rows, stress_row, 0)

    def fix_stress(s, where, c, halo, sign):
        at = where + (every,)
        d0, d1, d2 = (sign * halo[w] for w in range(waves))
        strain0[(s, c) + at] += d0
        second = shear[at]
        own_born = second * d1 + shear_change[at] * d0
        own_adjoint = second * d2
        if c >= 3:
            st[(s, 1, c) + at] += COURANT * own_born
            st[(s, 2, c) + at] += COURANT * own_adjoint
            return
        born = lame[at] * d1 + lame_change[at] * d0
        adjoint = lame[at] * d2
        for i in range(3):
            more_born, more_adjoint = born, adjoint
            if i == c:
                more_born, more_adjoint = born + 2.0 * own_born, adjoint + 2.0 * own_adjoint
            st[(s, 1, i) + at] += COURANT * more_born
            st[(s, 2, i) + at] += COURANT * more_adjoint

    for s in range(shots):
        (up_x_copy, _, up_x_in), (low_x_copy, _, low_x_in), (up_y_copy, _, up_y_in), (
            low_y_copy,
            _,
            low_y_in,
        ) = motion_faces[s]

        @pl.when(low_x_in)
        def _(s=s, copy=low_x_copy):
            copy.wait_recv()
            fix_stress(s, low_face, 0, layers(low_rows, s), -1.0)

        @pl.when(up_x_in)
        def _(s=s, copy=up_x_copy):
            copy.wait_recv()
            fix_stress(s, up_face, 3, layers(up_rows, s, 0), 1.0)
            fix_stress(s, up_face, 4, layers(up_rows, s, 1), 1.0)

        @pl.when(low_y_in)
        def _(s=s, copy=low_y_copy):
            copy.wait_recv()
            fix_stress(s, left_face, 1, layers(low_cols, s), -1.0)

        @pl.when(up_y_in)
        def _(s=s, copy=up_y_copy):
            copy.wait_recv()
            fix_stress(s, right_face, 3, layers(up_cols, s, 0), 1.0)
            fix_stress(s, right_face, 5, layers(up_cols, s, 1), 1.0)

    def term_row(x, carry):
        trace_sum, shear_sum = None, None
        for s in range(shots):
            e = [strain0[s, c, x] for c in range(6)]
            a = [st[s, 2, c, x] for c in range(6)]
            trace = (e[0] + e[1] + e[2]) * (a[0] + a[1] + a[2])
            product = (
                2.0 * (e[0] * a[0] + e[1] * a[1] + e[2] * a[2])
                + e[3] * a[3]
                + e[4] * a[4]
                + e[5] * a[5]
            )
            trace_sum = trace if s == 0 else trace_sum + trace
            shear_sum = product if s == 0 else shear_sum + product
        terms[0, x] = trace_sum
        terms[1, x] = shear_sum
        return carry

    shares = []
    for k in range(1, groups):
        peer = lax.rem(me + k, groups)
        lax.fori_loop(0, own, lambda i, carry, peer=peer: term_row(peer * own + i, carry), 0)
        copy = pltpu.make_async_remote_copy(
            src_ref=terms.at[:, pl.ds(peer * own, own)],
            dst_ref=landed.at[k - 1],
            send_sem=share_send_sem.at[k - 1],
            recv_sem=share_recv_sem.at[k - 1],
            device_id={"shot": peer},
            device_id_type=MESH,
        )
        copy.start()
        shares.append(copy)
    lax.fori_loop(0, own, lambda i, carry: term_row(me * own + i, carry), 0)
    for copy in shares:
        copy.wait_recv()
    total = terms[:, pl.ds(me * own, own)]
    for k in range(1, groups):
        total = total + landed[k - 1]
    kernels[...] = total * (1.0 / total_shots)
    for s in range(shots):
        sent(stress_faces[s])
        sent(motion_faces[s])
    for copy in shares:
        copy.wait_send()


def write_kernel(st, mo, kernels_in, new_velocity, new_stress, kernels, sems):
    shots = st.shape[0]
    copies = [pltpu.make_async_copy(kernels_in, kernels, sems.at[2 * shots])]
    for s in range(shots):
        copies.append(
            pltpu.make_async_copy(st.at[s, pl.ds(1, 2)], new_stress.at[s], sems.at[2 * s])
        )
        copies.append(
            pltpu.make_async_copy(mo.at[s, pl.ds(1, 2)], new_velocity.at[s], sems.at[2 * s + 1])
        )
    for copy in copies:
        copy.start()
    for copy in copies:
        copy.wait()


def shards(
    stress_fields,
    velocity_fields,
    lame,
    shear,
    density,
    lame_change,
    shear_change,
    density_change,
    source_cell,
    source_amp,
    receiver_cell,
):
    rows, cols, depth = lame.shape
    shots, waves = stress_fields.shape[:2]
    groups = lax.axis_size("shot")
    own = rows // groups
    every_column = cols * lax.axis_size("gy")
    f32 = jnp.float32
    hbm = pl.BlockSpec(memory_space=pltpu.HBM)
    smem = pl.BlockSpec(memory_space=pltpu.SMEM)
    vmem = pl.BlockSpec(memory_space=pltpu.VMEM)
    face_rows = [(shots, waves, cols, depth), (shots, waves, 2, cols, depth)]
    face_cols = [(shots, waves, rows, depth), (shots, waves, 2, rows, depth)]
    scratch = [
        (6, rows, cols, depth),
        None,
        (shots, rows, cols, depth),
        (shots, 3, rows, cols, depth),
        (shots, 6, rows, cols, depth),
        (3, rows, cols, depth),
        face_rows[0],
        face_rows[1],
        face_cols[0],
        face_cols[1],
        face_cols[0],
        face_cols[1],
        face_rows[1],
        face_rows[0],
        face_cols[1],
        face_cols[0],
        face_cols[1],
        face_cols[0],
        (max(groups - 1, 1), 3, own, cols, depth),
    ]
    scratch = [
        pltpu.VMEM(receiver_cell.shape, jnp.int32) if dims is None else pltpu.VMEM(dims, f32)
        for dims in scratch
    ]
    st, mo, kernels = pl.pallas_call(
        functools.partial(step_kernel, every_column, shots * groups),
        name="step",
        out_shape=(
            pltpu.VMEM((shots, waves, 6, rows, cols, depth), f32),
            pltpu.VMEM((shots, waves, 3, rows, cols, depth), f32),
            pltpu.VMEM((3, own, cols, depth), f32),
        ),
        in_specs=[hbm] * 9 + [smem] * 2,
        out_specs=(vmem, vmem, vmem),
        scratch_shapes=scratch
        + [
            pltpu.SemaphoreType.DMA((shots, 2)),
            pltpu.SemaphoreType.DMA((7,)),
            pltpu.SemaphoreType.DMA((8 * shots,)),
            pltpu.SemaphoreType.DMA((8 * shots,)),
            pltpu.SemaphoreType.DMA((max(groups - 1, 1),)),
            pltpu.SemaphoreType.DMA((max(groups - 1, 1),)),
        ],
        compiler_params=pltpu.CompilerParams(
            collective_id=0, has_side_effects=True, vmem_limit_bytes=VMEM_LIMIT
        ),
    )(
        *(
            pltpu.with_memory_space_constraint(array, pltpu.HBM)
            for array in (
                stress_fields,
                velocity_fields,
                lame,
                shear,
                density,
                lame_change,
                shear_change,
                density_change,
                receiver_cell,
                source_cell,
                source_amp,
            )
        ),
    )
    shape = lambda *dims: jax.ShapeDtypeStruct(dims, f32)
    return pl.pallas_call(
        write_kernel,
        name="write",
        out_shape=(
            shape(shots, 2, 3, rows, cols, depth),
            shape(shots, 2, 6, rows, cols, depth),
            shape(3, own, cols, depth),
        ),
        in_specs=[vmem] * 3,
        out_specs=(hbm, hbm, hbm),
        scratch_shapes=[pltpu.SemaphoreType.DMA((2 * shots + 1,))],
        compiler_params=pltpu.CompilerParams(vmem_limit_bytes=VMEM_LIMIT),
    )(st, mo, kernels)


def solution(mesh):
    return jax.shard_map(
        shards,
        mesh=mesh,
        in_specs=(
            P("shot", None, None, "gx", "gy", None),
            P("shot", None, None, "gx", "gy", None),
            P("gx", "gy", None),
            P("gx", "gy", None),
            P("gx", "gy", None),
            P("gx", "gy", None),
            P("gx", "gy", None),
            P("gx", "gy", None),
            P("shot"),
            P("shot"),
            P("shot", None),
        ),
        out_specs=(
            P("shot", None, None, "gx", "gy", None),
            P("shot", None, None, "gx", "gy", None),
            P(None, ("gx", "shot"), "gy", None),
        ),
        check_vma=False,
    )
```

time: 29.2 us -> 18 us (0.62)
  Pallas kernels: 26.8 us -> 17.2 us
  local copies, waits for them, and re-layouts: 1.62 us -> 0 us
    pallas_call x3 -> x2, Pallas kernels: 26.8 us -> 17.2 us  [the longest x1 15 us: shards(): pl.pallas_call(functools.partial(step_kernel, every_column, shots * group...]
    unnamed x1 -> x0, local copies, waits for them, and re-layouts: 1.62 us -> none
where the time goes in v2:
time: 18 us; the launch traced here: 17.9 us
  Pallas kernels  17.2 us (96%)
  between operations  0.64 us (4%)
    pallas_call x1, Pallas kernels, shards(): pl.pallas_call(functools.partial(step_kernel, every_column, shots * group...  15 us
    pallas_call x1, Pallas kernels, shards(): pl.pallas_call(write_kernel, name='write', out_shape=(shape(shots, 2, 3,...  2.28 us

profile of v2, /device:TPU:0, one launch (start us, length us, event | category | flops | bytes accessed | tf_op | source)
XLA Modules:
  0.0 17.9 jit_solution(825249613896320829)
XLA Ops:
  0.6 15.0 %step.1 = (f32[2,3,6,16,16,128]{5,4,3,2,1,0:T(8,128)S(1)}, f32[2,3,3,16,16,128]{5,4,3,2,1,0:T(8,128)S(1)}, f32[3,8,16,128]{3,2,1,0:T(8,128)S(1)}) custom-call(f32[2,3,6,16,16,128]{5,4,3,2,1,0:T(8,128)} %stress.1, f32[2,3,3,16,16,128]{5,4,3,2,1,0:T(8,128)} %velocity.1, f32[16,16,128]{2,1,0:T(8,128)} %lame_in.1, f32[16,16,128]{2,1,0:T(8,128)} %shear_in.1, ...), custom_call_target="tpu_custom_call" | custom-call | tf_op jit(solution)/shard_map/step/pallas_call | solution.py:526
  15.6 2.3 %write.1 = (f32[2,2,3,16,16,128]{5,4,3,2,1,0:T(8,128)}, f32[2,2,6,16,16,128]{5,4,3,2,1,0:T(8,128)}, f32[3,8,16,128]{3,2,1,0:T(8,128)}) custom-call(f32[2,3,6,16,16,128]{5,4,3,2,1,0:T(8,128)S(1)} %get-tuple-element.6.st, f32[2,3,3,16,16,128]{5,4,3,2,1,0:T(8,128)S(1)} %get-tuple-element.7.mo, f32[3,8,16,128]{3,2,1,0:T(8,128)S(1)} %get-tuple-element.8.kernels_in), custom_call_target="tpu_custom_call" | custom-call | tf_op jit(solution)/shard_map/write/pallas_call | solution.py:567

commit v3 on v2

--- a/solution.py
+++ b/solution.py
@@ -248,7 +248,7 @@
                 mo[s, 2, c, x] = adjoint
             return carry
 
-        lax.fori_loop(0, rows, motion_row, 0)
+        lax.fori_loop(0, rows, motion_row, 0, unroll=2)
 
     every = slice(None)
     low_face, up_face = (0, every), (rows - 1, every)
@@ -361,7 +361,7 @@
             terms[2, x] = total if s == 0 else terms[2, x] + total
             return carry
 
-        lax.fori_loop(0, rows, stress_row, 0)
+        lax.fori_loop(0, rows, stress_row, 0, unroll=2)
 
     def fix_stress(s, where, c, halo, sign):
         at = where + (every,)
@@ -433,7 +433,7 @@
     shares = []
     for k in range(1, groups):
         peer = lax.rem(me + k, groups)
-        lax.fori_loop(0, own, lambda i, carry, peer=peer: term_row(peer * own + i, carry), 0)
+        lax.fori_loop(0, own, lambda i, carry, peer=peer: term_row(peer * own + i, carry), 0, unroll=2)
         copy = pltpu.make_async_remote_copy(
             src_ref=terms.at[:, pl.ds(peer * own, own)],
             dst_ref=landed.at[k - 1],
@@ -444,7 +444,7 @@
         )
         copy.start()
         shares.append(copy)
-    lax.fori_loop(0, own, lambda i, carry: term_row(me * own + i, carry), 0)
+    lax.fori_loop(0, own, lambda i, carry: term_row(me * own + i, carry), 0, unroll=2)
     for copy in shares:
         copy.wait_recv()
     total = terms[:, pl.ds(me * own, own)]

time: 18 us -> 17.1 us (0.950)
  Pallas kernels: 17.2 us -> 16.3 us
    pallas_call x1, Pallas kernels: 15 us -> 14.1 us  [shards(): pl.pallas_call(functools.partial(step_kernel, every_column, shots * group...]
where the time goes in v3:
time: 17.1 us; the launch traced here: 17 us
  Pallas kernels  16.3 us (95%)
  between operations  0.64 us (4%)
    pallas_call x1, Pallas kernels, shards(): pl.pallas_call(functools.partial(step_kernel, every_column, shots * group...  14.1 us
    pallas_call x1, Pallas kernels, shards(): pl.pallas_call(write_kernel, name='write', out_shape=(shape(shots, 2, 3,...  2.28 us

profile of v3, /device:TPU:0, one launch (start us, length us, event | category | flops | bytes accessed | tf_op | source)
XLA Modules:
  0.0 17.0 jit_solution(15632607633024056783)
XLA Ops:
  0.6 14.1 %step.1 = (f32[2,3,6,16,16,128]{5,4,3,2,1,0:T(8,128)S(1)}, f32[2,3,3,16,16,128]{5,4,3,2,1,0:T(8,128)S(1)}, f32[3,8,16,128]{3,2,1,0:T(8,128)S(1)}) custom-call(f32[2,3,6,16,16,128]{5,4,3,2,1,0:T(8,128)} %stress.1, f32[2,3,3,16,16,128]{5,4,3,2,1,0:T(8,128)} %velocity.1, f32[16,16,128]{2,1,0:T(8,128)} %lame_in.1, f32[16,16,128]{2,1,0:T(8,128)} %shear_in.1, ...), custom_call_target="tpu_custom_call" | custom-call | tf_op jit(solution)/shard_map/step/pallas_call | solution.py:526
  14.7 2.3 %write.1 = (f32[2,2,3,16,16,128]{5,4,3,2,1,0:T(8,128)}, f32[2,2,6,16,16,128]{5,4,3,2,1,0:T(8,128)}, f32[3,8,16,128]{3,2,1,0:T(8,128)}) custom-call(f32[2,3,6,16,16,128]{5,4,3,2,1,0:T(8,128)S(1)} %get-tuple-element.6.st, f32[2,3,3,16,16,128]{5,4,3,2,1,0:T(8,128)S(1)} %get-tuple-element.7.mo, f32[3,8,16,128]{3,2,1,0:T(8,128)S(1)} %get-tuple-element.8.kernels_in), custom_call_target="tpu_custom_call" | custom-call | tf_op jit(solution)/shard_map/write/pallas_call | solution.py:567

commit v4 on v3

--- a/solution.py
+++ b/solution.py
@@ -281,29 +281,31 @@
             low_y_in,
         ) = stress_faces[s]
 
+        @pl.when(up_y_in)
+        def _(s=s, copy=up_y_copy):
+            copy.wait_recv()
+            fix_motion(s, right_face, 1, layers(st_up_cols, s), 1.0)
+
+        @pl.when(low_y_in)
+        def _(s=s, copy=low_y_copy):
+            copy.wait_recv()
+            fix_motion(s, left_face, 0, layers(st_low_cols, s, 0), -1.0)
+            fix_motion(s, left_face, 2, layers(st_low_cols, s, 1), -1.0)
+
         @pl.when(up_x_in)
         def _(s=s, copy=up_x_copy):
             copy.wait_recv()
             fix_motion(s, up_face, 0, layers(st_up_rows, s), 1.0)
 
+        send(motion_faces[s][1:2])
+
         @pl.when(low_x_in)
         def _(s=s, copy=low_x_copy):
             copy.wait_recv()
             fix_motion(s, low_face, 1, layers(st_low_rows, s, 0), -1.0)
             fix_motion(s, low_face, 2, layers(st_low_rows, s, 1), -1.0)
 
-        @pl.when(up_y_in)
-        def _(s=s, copy=up_y_copy):
-            copy.wait_recv()
-            fix_motion(s, right_face, 1, layers(st_up_cols, s), 1.0)
-
-        @pl.when(low_y_in)
-        def _(s=s, copy=low_y_copy):
-            copy.wait_recv()
-            fix_motion(s, left_face, 0, layers(st_low_cols, s, 0), -1.0)
-            fix_motion(s, left_face, 2, layers(st_low_cols, s, 1), -1.0)
-
-        send(motion_faces[s][:2])
+        send(motion_faces[s][:1])
         for w in range(waves):
             up_cols_out[s, w, 0] = mo[s, w, 0, :, 0, :]
             up_cols_out[s, w, 1] = mo[s, w, 2, :, 0, :]

time: 17.1 us -> 17.2 us (level)
  no operation moved by 1% of the time
where the time goes in v4:
time: 17.2 us; the launch traced here: 17 us
  Pallas kernels  16.4 us (95%)
  between operations  0.64 us (4%)
    pallas_call x1, Pallas kernels, shards(): pl.pallas_call(functools.partial(step_kernel, every_column, shots * group...  14.1 us
    pallas_call x1, Pallas kernels, shards(): pl.pallas_call(write_kernel, name='write', out_shape=(shape(shots, 2, 3,...  2.28 us

profile of v4, /device:TPU:0, one launch (start us, length us, event | category | flops | bytes accessed | tf_op | source)
XLA Modules:
  0.0 17.0 jit_solution(4652641003332854718)
XLA Ops:
  0.6 14.1 %step.1 = (f32[2,3,6,16,16,128]{5,4,3,2,1,0:T(8,128)S(1)}, f32[2,3,3,16,16,128]{5,4,3,2,1,0:T(8,128)S(1)}, f32[3,8,16,128]{3,2,1,0:T(8,128)S(1)}) custom-call(f32[2,3,6,16,16,128]{5,4,3,2,1,0:T(8,128)} %stress.1, f32[2,3,3,16,16,128]{5,4,3,2,1,0:T(8,128)} %velocity.1, f32[16,16,128]{2,1,0:T(8,128)} %lame_in.1, f32[16,16,128]{2,1,0:T(8,128)} %shear_in.1, ...), custom_call_target="tpu_custom_call" | custom-call | tf_op jit(solution)/shard_map/step/pallas_call | solution.py:528
  14.8 2.3 %write.1 = (f32[2,2,3,16,16,128]{5,4,3,2,1,0:T(8,128)}, f32[2,2,6,16,16,128]{5,4,3,2,1,0:T(8,128)}, f32[3,8,16,128]{3,2,1,0:T(8,128)}) custom-call(f32[2,3,6,16,16,128]{5,4,3,2,1,0:T(8,128)S(1)} %get-tuple-element.6.st, f32[2,3,3,16,16,128]{5,4,3,2,1,0:T(8,128)S(1)} %get-tuple-element.7.mo, f32[3,8,16,128]{3,2,1,0:T(8,128)S(1)} %get-tuple-element.8.kernels_in), custom_call_target="tpu_custom_call" | custom-call | tf_op jit(solution)/shard_map/write/pallas_call | solution.py:569
